TPU v7x, 128 devices: a whole 4x4x4 slice. The times are simulated.
128 devices in a mesh: row: 32 (over y_hi, x, z), rep: 4 (over y_lo, core).
Axes of the slice: x: 4, y: 4 (y_hi: 2, y_lo: 2; y = y_hi * 2 + y_lo), z: 4, core: 2. Of those that a mesh axis runs over, the one named last changes fastest.
Arguments:
- features: bfloat16 [16384, 256], P('row'), may hold values from -6 to 6
- weight: bfloat16 [256, 256], replicated, may hold values from -0.375 to 0.375
- adj_tiles: bfloat16 [128, 64, 128, 128], P('row', 'rep'), as said below
- block_cols: int32 [128, 64], P('row', 'rep'), may hold values from 0 to 127, as said below
- edge_keep: int32 [128, 64], P('row', 'rep'), may hold values 0 or 1
- drop_key: int32 [2], replicated, may hold values from 0 to 1048575
- cotangent: bfloat16 [16384, 256], P('row'), may hold values from -6 to 6
Outputs:
- hidden: bfloat16 [16384, 256], P('row')
- weight_grad: float32 [256, 256], replicated
- feature_grad: bfloat16 [16384, 256], P(('row', 'rep'))
Inputs may be any that keep to these rules, and one draw needn't show every extreme that they name: For slot k of block row i, the group block_cols[i, k] // 4 is congruent to i // 4 - k // 16 modulo 4. `adj_tiles`: entries are zero or positive.
All inputs are finite; a program needn't handle non-finite values. No bound on the sum of `edge_keep` on one device may be relied on, other than what follows from the above.
Results may differ from a plain program's by a relative error of at most 0.022.
Values may be sent and summed in bfloat16 or wider, within the bound.
A program may use at most 64 MiB of HBM per device.

v0:
```python
import jax
import jax.numpy as jnp
from jax import lax
from jax.sharding import PartitionSpec as P


def from_behind(shard, axis, by):
    devices = lax.axis_size(axis)
    return lax.ppermute(shard, axis, [(i, (i + by) % devices) for i in range(devices)])


def keep_mask(node_ids, feat_ids, drop_key):
    mixed_hash = node_ids * 73856093 ^ feat_ids * 19349663 ^ drop_key[0] * 83492791 ^ drop_key[1]
    mixed_hash = mixed_hash ^ lax.shift_right_logical(mixed_hash, jnp.int32(13))
    mixed_hash = mixed_hash * 1274126177
    mixed_hash = mixed_hash ^ lax.shift_right_logical(mixed_hash, jnp.int32(16))
    return mixed_hash & 1023 < 819


def shards(features, weight, adj_tiles, block_cols, edge_keep, drop_key, cotangent):
    panel_rows, feat_dim = features.shape
    per_group, slot_count = block_cols.shape
    block_size = adj_tiles.shape[2]
    cycle_size = lax.axis_size("row")
    rep_size = lax.axis_size("rep")
    row_index = lax.axis_index("row")
    rep_index = lax.axis_index("rep")
    block_total = cycle_size * per_group
    node_ids = row_index * panel_rows + lax.broadcasted_iota(jnp.int32, (panel_rows, feat_dim), 0)
    feat_ids = lax.broadcasted_iota(jnp.int32, (panel_rows, feat_dim), 1)
    kept_mask = keep_mask(node_ids, feat_ids, drop_key)
    masked = jnp.where(kept_mask, features, jnp.zeros_like(features))
    gated_tiles = adj_tiles * edge_keep[:, :, None, None].astype(jnp.bfloat16)
    flat_cols = block_cols.reshape(-1)
    col_part = jnp.sum(gated_tiles, axis=2, dtype=jnp.float32).reshape(
        per_group * slot_count, block_size
    )
    row_part = jnp.sum(gated_tiles, axis=(1, 3), dtype=jnp.float32)
    onehot_cols = (flat_cols[:, None] == jnp.arange(block_total, dtype=jnp.int32)[None, :]).astype(
        jnp.float32
    )
    col_full = jnp.einsum("sn,sb->nb", onehot_cols, col_part, precision=lax.Precision.HIGHEST)
    own_start = row_index * per_group
    row_full = lax.dynamic_update_slice_in_dim(
        jnp.zeros((block_total, block_size), jnp.float32), row_part, own_start, 0
    )
    col_total, row_total = lax.psum((col_full, row_full), ("row", "rep"))
    col_scale = lax.rsqrt(
        1.0 + lax.dynamic_slice_in_dim(col_total, own_start, per_group, 0)
    ).reshape(panel_rows, 1)
    row_scale = lax.rsqrt(
        1.0 + lax.dynamic_slice_in_dim(row_total, own_start, per_group, 0)
    ).reshape(panel_rows, 1)
    scaled = (
        jnp.dot(masked, weight, preferred_element_type=jnp.float32) * 1.25 * col_scale
    ).astype(jnp.bfloat16)
    proj_panel = scaled.reshape(per_group, block_size, feat_dim)
    group_of = flat_cols // per_group
    within = flat_cols - group_of * per_group

    def every_section(section_idx, state_pair):
        held_panel, stack = state_pair
        stack = lax.dynamic_update_index_in_dim(stack, held_panel, section_idx, 0)
        held_panel = from_behind(held_panel, "row", 1)
        return (held_panel, stack)

    stack = jnp.zeros((cycle_size, per_group, block_size, feat_dim), jnp.bfloat16)
    held_panel, stack = lax.fori_loop(0, cycle_size - 1, every_section, (proj_panel, stack))
    stack = lax.dynamic_update_index_in_dim(stack, held_panel, cycle_size - 1, 0)
    section_of = jnp.mod(row_index - group_of, cycle_size)
    flat_stack = stack.reshape(-1, block_size, feat_dim)
    chosen = flat_stack[section_of * per_group + within]
    chosen = chosen.reshape(per_group, slot_count, block_size, feat_dim)
    summed_local = jnp.einsum(
        "ikab,ikbf->iaf", gated_tiles, chosen, preferred_element_type=jnp.float32
    )
    summed = lax.psum(summed_local.astype(jnp.bfloat16), "rep").astype(jnp.float32)
    row_block = row_scale.reshape(per_group, block_size, 1)
    preact = row_block * (summed + proj_panel.astype(jnp.float32))
    sigmoid_val = jax.nn.sigmoid(preact)
    hidden = (preact * sigmoid_val).astype(jnp.bfloat16).reshape(panel_rows, feat_dim)
    pre_grad = cotangent.astype(jnp.float32).reshape(per_group, block_size, feat_dim)
    pre_grad = pre_grad * sigmoid_val * (1.0 + preact * (1.0 - sigmoid_val))
    self_term = pre_grad * row_block
    pushed = self_term.astype(jnp.bfloat16)
    contribution = jnp.einsum(
        "ikab,iaf->ikbf", gated_tiles, pushed, preferred_element_type=jnp.float32
    )
    contribution = contribution.reshape(per_group * slot_count, block_size, feat_dim)
    share_rows = panel_rows // rep_size
    row_count = panel_rows * lax.axis_size("row")
    block_count = row_count // block_size
    onehot = (flat_cols[:, None] == jnp.arange(block_count, dtype=jnp.int32)[None, :]).astype(
        jnp.float32
    )
    spread = jnp.einsum("sn,sbf->nbf", onehot, contribution, precision=lax.Precision.HIGHEST)
    group_part = lax.psum_scatter(
        spread.reshape(row_count, feat_dim).astype(jnp.bfloat16),
        "row",
        scatter_dimension=0,
        tiled=True,
    )
    transposed = lax.psum_scatter(group_part, "rep", scatter_dimension=0, tiled=True).astype(
        jnp.float32
    )
    share_start = rep_index * share_rows
    self_share = lax.dynamic_slice_in_dim(
        self_term.reshape(panel_rows, feat_dim), share_start, share_rows, 0
    )
    col_share = lax.dynamic_slice_in_dim(col_scale, share_start, share_rows, 0)
    proj_grad = (col_share * (self_share + transposed)).astype(jnp.bfloat16)
    masked_share = lax.dynamic_slice_in_dim(masked, share_start, share_rows, 0)
    kept_share = lax.dynamic_slice_in_dim(kept_mask, share_start, share_rows, 0)
    weight_local = (
        lax.dot_general(
            masked_share, proj_grad, (((0,), (0,)), ((), ())), preferred_element_type=jnp.float32
        )
        * 1.25
    )
    weight_grad = lax.psum(weight_local, ("row", "rep"))
    back_proj = (
        lax.dot_general(
            proj_grad, weight, (((1,), (1,)), ((), ())), preferred_element_type=jnp.float32
        )
        * 1.25
    )
    feature_grad = jnp.where(kept_share, back_proj, jnp.zeros_like(back_proj)).astype(jnp.bfloat16)
    return (hidden, weight_grad, feature_grad)


def solution(mesh):
    in_specs = (
        P("row", None),
        P(),
        P("row", "rep", None, None),
        P("row", "rep"),
        P("row", "rep"),
        P(),
        P("row", None),
    )
    out_specs = (P("row", None), P(), P(("row", "rep"), None))
    return jax.shard_map(shards, mesh=mesh, in_specs=in_specs, out_specs=out_specs, check_vma=False)
```

profile of v0, /device:TPU:1, one launch (start us, length us, event | category | flops | bytes accessed | tf_op | source)
XLA Modules:
  0.0 1006.7 jit_solution(13910474212543994643)
XLA Ops:
  17.5 139.6 %all-reduce.9.cloned.1.call-done = (f32[128,128]{1,0:T(8,128)}, f32[128,128]{1,0:T(8,128)}) async-done(((f32[128,128]{1,0:T(8,128)}, f32[128,128]{1,0:T(8,128)}), (f32[128,128]{1,0:T(8,128)}, f32[128,128]{1,0:T(8,128)})) %all-reduce.9.cloned.1.call-update) | async-done | bytes 131088 | tf_op jit(solution)/shard_map/psum | solution.py:47
  162.9 361.8 %while.15 = (s32[]{:T(128)}, bf16[4,128,256]{2,1,0:T(8,128)(2,1)S(1)}, bf16[32,4,128,256]{3,2,1,0:T(8,128)(2,1)}, s32[]{:T(128)}) while((s32[]{:T(128)}, bf16[4,128,256]{2,1,0:T(8,128)(2,1)S(1)}, bf16[32,4,128,256]{3,2,1,0:T(8,128)(2,1)}, s32[]{:T(128)}) %tuple.36), condition=%wide.region_5.6_spmd, body=%wide.region_4.5_spmd.sunk | while | flops 2 | bytes 2097257 | solution.py:68
  164.6 10.7 %collective-permute-done = bf16[4,128,256]{2,1,0:T(8,128)(2,1)S(1)} collective-permute-done((bf16[4,128,256]{2,1,0:T(8,128)(2,1)S(1)}, bf16[4,128,256]{2,1,0:T(8,128)(2,1)S(1)}, u32[]{:S(2)}, u32[]{:S(2)}) %collective-permute-start) | collective-permute-done | bytes 262176 | tf_op jit(solution)/shard_map/while/body/eval_jaxpr/ppermute | solution.py:9
  176.2 10.6 %collective-permute-done = bf16[4,128,256]{2,1,0:T(8,128)(2,1)S(1)} collective-permute-done((bf16[4,128,256]{2,1,0:T(8,128)(2,1)S(1)}, bf16[4,128,256]{2,1,0:T(8,128)(2,1)S(1)}, u32[]{:S(2)}, u32[]{:S(2)}) %collective-permute-start) | collective-permute-done | bytes 262176 | tf_op jit(solution)/shard_map/while/body/eval_jaxpr/ppermute | solution.py:9
  198.7 10.2 %collective-permute-done = bf16[4,128,256]{2,1,0:T(8,128)(2,1)S(1)} collective-permute-done((bf16[4,128,256]{2,1,0:T(8,128)(2,1)S(1)}, bf16[4,128,256]{2,1,0:T(8,128)(2,1)S(1)}, u32[]{:S(2)}, u32[]{:S(2)}) %collective-permute-start) | collective-permute-done | bytes 262176 | tf_op jit(solution)/shard_map/while/body/eval_jaxpr/ppermute | solution.py:9
  220.7 10.2 %collective-permute-done = bf16[4,128,256]{2,1,0:T(8,128)(2,1)S(1)} collective-permute-done((bf16[4,128,256]{2,1,0:T(8,128)(2,1)S(1)}, bf16[4,128,256]{2,1,0:T(8,128)(2,1)S(1)}, u32[]{:S(2)}, u32[]{:S(2)}) %collective-permute-start) | collective-permute-done | bytes 262176 | tf_op jit(solution)/shard_map/while/body/eval_jaxpr/ppermute | solution.py:9
  231.8 10.2 %collective-permute-done = bf16[4,128,256]{2,1,0:T(8,128)(2,1)S(1)} collective-permute-done((bf16[4,128,256]{2,1,0:T(8,128)(2,1)S(1)}, bf16[4,128,256]{2,1,0:T(8,128)(2,1)S(1)}, u32[]{:S(2)}, u32[]{:S(2)}) %collective-permute-start) | collective-permute-done | bytes 262176 | tf_op jit(solution)/shard_map/while/body/eval_jaxpr/ppermute | solution.py:9
  253.8 11.2 %collective-permute-done = bf16[4,128,256]{2,1,0:T(8,128)(2,1)S(1)} collective-permute-done((bf16[4,128,256]{2,1,0:T(8,128)(2,1)S(1)}, bf16[4,128,256]{2,1,0:T(8,128)(2,1)S(1)}, u32[]{:S(2)}, u32[]{:S(2)}) %collective-permute-start) | collective-permute-done | bytes 262176 | tf_op jit(solution)/shard_map/while/body/eval_jaxpr/ppermute | solution.py:9
  265.9 12.3 %collective-permute-done = bf16[4,128,256]{2,1,0:T(8,128)(2,1)S(1)} collective-permute-done((bf16[4,128,256]{2,1,0:T(8,128)(2,1)S(1)}, bf16[4,128,256]{2,1,0:T(8,128)(2,1)S(1)}, u32[]{:S(2)}, u32[]{:S(2)}) %collective-permute-start) | collective-permute-done | bytes 262176 | tf_op jit(solution)/shard_map/while/body/eval_jaxpr/ppermute | solution.py:9
  279.1 12.9 %collective-permute-done = bf16[4,128,256]{2,1,0:T(8,128)(2,1)S(1)} collective-permute-done((bf16[4,128,256]{2,1,0:T(8,128)(2,1)S(1)}, bf16[4,128,256]{2,1,0:T(8,128)(2,1)S(1)}, u32[]{:S(2)}, u32[]{:S(2)}) %collective-permute-start) | collective-permute-done | bytes 262176 | tf_op jit(solution)/shard_map/while/body/eval_jaxpr/ppermute | solution.py:9
  292.8 12.0 %collective-permute-done = bf16[4,128,256]{2,1,0:T(8,128)(2,1)S(1)} collective-permute-done((bf16[4,128,256]{2,1,0:T(8,128)(2,1)S(1)}, bf16[4,128,256]{2,1,0:T(8,128)(2,1)S(1)}, u32[]{:S(2)}, u32[]{:S(2)}) %collective-permute-start) | collective-permute-done | bytes 262176 | tf_op jit(solution)/shard_map/while/body/eval_jaxpr/ppermute | solution.py:9
  305.6 11.1 %collective-permute-done = bf16[4,128,256]{2,1,0:T(8,128)(2,1)S(1)} collective-permute-done((bf16[4,128,256]{2,1,0:T(8,128)(2,1)S(1)}, bf16[4,128,256]{2,1,0:T(8,128)(2,1)S(1)}, u32[]{:S(2)}, u32[]{:S(2)}) %collective-permute-start) | collective-permute-done | bytes 262176 | tf_op jit(solution)/shard_map/while/body/eval_jaxpr/ppermute | solution.py:9
  328.5 10.2 %collective-permute-done = bf16[4,128,256]{2,1,0:T(8,128)(2,1)S(1)} collective-permute-done((bf16[4,128,256]{2,1,0:T(8,128)(2,1)S(1)}, bf16[4,128,256]{2,1,0:T(8,128)(2,1)S(1)}, u32[]{:S(2)}, u32[]{:S(2)}) %collective-permute-start) | collective-permute-done | bytes 262176 | tf_op jit(solution)/shard_map/while/body/eval_jaxpr/ppermute | solution.py:9
  339.6 10.2 %collective-permute-done = bf16[4,128,256]{2,1,0:T(8,128)(2,1)S(1)} collective-permute-done((bf16[4,128,256]{2,1,0:T(8,128)(2,1)S(1)}, bf16[4,128,256]{2,1,0:T(8,128)(2,1)S(1)}, u32[]{:S(2)}, u32[]{:S(2)}) %collective-permute-start) | collective-permute-done | bytes 262176 | tf_op jit(solution)/shard_map/while/body/eval_jaxpr/ppermute | solution.py:9
  350.6 10.2 %collective-permute-done = bf16[4,128,256]{2,1,0:T(8,128)(2,1)S(1)} collective-permute-done((bf16[4,128,256]{2,1,0:T(8,128)(2,1)S(1)}, bf16[4,128,256]{2,1,0:T(8,128)(2,1)S(1)}, u32[]{:S(2)}, u32[]{:S(2)}) %collective-permute-start) | collective-permute-done | bytes 262176 | tf_op jit(solution)/shard_map/while/body/eval_jaxpr/ppermute | solution.py:9
  383.7 10.8 %collective-permute-done = bf16[4,128,256]{2,1,0:T(8,128)(2,1)S(1)} collective-permute-done((bf16[4,128,256]{2,1,0:T(8,128)(2,1)S(1)}, bf16[4,128,256]{2,1,0:T(8,128)(2,1)S(1)}, u32[]{:S(2)}, u32[]{:S(2)}) %collective-permute-start) | collective-permute-done | bytes 262176 | tf_op jit(solution)/shard_map/while/body/eval_jaxpr/ppermute | solution.py:9
  395.4 11.9 %collective-permute-done = bf16[4,128,256]{2,1,0:T(8,128)(2,1)S(1)} collective-permute-done((bf16[4,128,256]{2,1,0:T(8,128)(2,1)S(1)}, bf16[4,128,256]{2,1,0:T(8,128)(2,1)S(1)}, u32[]{:S(2)}, u32[]{:S(2)}) %collective-permute-start) | collective-permute-done | bytes 262176 | tf_op jit(solution)/shard_map/while/body/eval_jaxpr/ppermute | solution.py:9
  408.1 13.3 %collective-permute-done = bf16[4,128,256]{2,1,0:T(8,128)(2,1)S(1)} collective-permute-done((bf16[4,128,256]{2,1,0:T(8,128)(2,1)S(1)}, bf16[4,128,256]{2,1,0:T(8,128)(2,1)S(1)}, u32[]{:S(2)}, u32[]{:S(2)}) %collective-permute-start) | collective-permute-done | bytes 262176 | tf_op jit(solution)/shard_map/while/body/eval_jaxpr/ppermute | solution.py:9
  422.2 12.5 %collective-permute-done = bf16[4,128,256]{2,1,0:T(8,128)(2,1)S(1)} collective-permute-done((bf16[4,128,256]{2,1,0:T(8,128)(2,1)S(1)}, bf16[4,128,256]{2,1,0:T(8,128)(2,1)S(1)}, u32[]{:S(2)}, u32[]{:S(2)}) %collective-permute-start) | collective-permute-done | bytes 262176 | tf_op jit(solution)/shard_map/while/body/eval_jaxpr/ppermute | solution.py:9
  435.5 11.5 %collective-permute-done = bf16[4,128,256]{2,1,0:T(8,128)(2,1)S(1)} collective-permute-done((bf16[4,128,256]{2,1,0:T(8,128)(2,1)S(1)}, bf16[4,128,256]{2,1,0:T(8,128)(2,1)S(1)}, u32[]{:S(2)}, u32[]{:S(2)}) %collective-permute-start) | collective-permute-done | bytes 262176 | tf_op jit(solution)/shard_map/while/body/eval_jaxpr/ppermute | solution.py:9
  447.9 10.6 %collective-permute-done = bf16[4,128,256]{2,1,0:T(8,128)(2,1)S(1)} collective-permute-done((bf16[4,128,256]{2,1,0:T(8,128)(2,1)S(1)}, bf16[4,128,256]{2,1,0:T(8,128)(2,1)S(1)}, u32[]{:S(2)}, u32[]{:S(2)}) %collective-permute-start) | collective-permute-done | bytes 262176 | tf_op jit(solution)/shard_map/while/body/eval_jaxpr/ppermute | solution.py:9
  459.3 10.2 %collective-permute-done = bf16[4,128,256]{2,1,0:T(8,128)(2,1)S(1)} collective-permute-done((bf16[4,128,256]{2,1,0:T(8,128)(2,1)S(1)}, bf16[4,128,256]{2,1,0:T(8,128)(2,1)S(1)}, u32[]{:S(2)}, u32[]{:S(2)}) %collective-permute-start) | collective-permute-done | bytes 262176 | tf_op jit(solution)/shard_map/while/body/eval_jaxpr/ppermute | solution.py:9
  470.3 10.2 %collective-permute-done = bf16[4,128,256]{2,1,0:T(8,128)(2,1)S(1)} collective-permute-done((bf16[4,128,256]{2,1,0:T(8,128)(2,1)S(1)}, bf16[4,128,256]{2,1,0:T(8,128)(2,1)S(1)}, u32[]{:S(2)}, u32[]{:S(2)}) %collective-permute-start) | collective-permute-done | bytes 262176 | tf_op jit(solution)/shard_map/while/body/eval_jaxpr/ppermute | solution.py:9
  492.4 10.2 %collective-permute-done = bf16[4,128,256]{2,1,0:T(8,128)(2,1)S(1)} collective-permute-done((bf16[4,128,256]{2,1,0:T(8,128)(2,1)S(1)}, bf16[4,128,256]{2,1,0:T(8,128)(2,1)S(1)}, u32[]{:S(2)}, u32[]{:S(2)}) %collective-permute-start) | collective-permute-done | bytes 262176 | tf_op jit(solution)/shard_map/while/body/eval_jaxpr/ppermute | solution.py:9
  503.4 10.2 %collective-permute-done = bf16[4,128,256]{2,1,0:T(8,128)(2,1)S(1)} collective-permute-done((bf16[4,128,256]{2,1,0:T(8,128)(2,1)S(1)}, bf16[4,128,256]{2,1,0:T(8,128)(2,1)S(1)}, u32[]{:S(2)}, u32[]{:S(2)}) %collective-permute-start) | collective-permute-done | bytes 262176 | tf_op jit(solution)/shard_map/while/body/eval_jaxpr/ppermute | solution.py:9
  514.5 10.2 %collective-permute-done = bf16[4,128,256]{2,1,0:T(8,128)(2,1)S(1)} collective-permute-done((bf16[4,128,256]{2,1,0:T(8,128)(2,1)S(1)}, bf16[4,128,256]{2,1,0:T(8,128)(2,1)S(1)}, u32[]{:S(2)}, u32[]{:S(2)}) %collective-permute-start) | collective-permute-done | bytes 262176 | tf_op jit(solution)/shard_map/while/body/eval_jaxpr/ppermute | solution.py:9
  536.3 66.6 %all-reduce.5.cloned.1.call-done = bf16[4,128,256]{2,1,0:T(8,128)(2,1)} async-done(((bf16[4,128,256]{2,1,0:T(8,128)(2,1)}), bf16[4,128,256]{2,1,0:T(8,128)(2,1)}) %all-reduce.5.cloned.1.call-update) | async-done | bytes 262160 | tf_op jit(solution)/shard_map/psum | solution.py:77
  606.8 13.4 %fusion.2 = bf16[128,128,256]{2,0,1:T(8,128)(2,1)} fusion(f32[64,128,256]{2,1,0:T(8,128)S(1)} %bitcast.43, s32[64]{0:T(128)S(1)} %eq.10), kind=kOutput, calls=%fused_computation.4 | convolution fusion | flops 3225427968 | bytes 16777472 | tf_op jit(solution)/shard_map/sn,sbf->nbf/dot_general | solution.py:96
  620.2 11.4 %copy.14 = bf16[128,128,256]{2,1,0:T(8,128)(2,1)} copy(bf16[128,128,256]{2,0,1:T(8,128)(2,1)} %fusion.2) | data formatting | bytes 16777216 | tf_op jit(solution)/shard_map/convert_element_type | solution.py:98
  631.7 180.7 %reduce-scatter.3.cloned.1.call-done = bf16[512,256]{1,0:T(8,128)(2,1)} async-done(((bf16[16384,256]{1,0:T(8,128)(2,1)}), bf16[512,256]{1,0:T(8,128)(2,1)}) %reduce-scatter.3.cloned.1.call-update) | async-done | bytes 262160 | tf_op jit(solution)/shard_map/reduce_scatter | solution.py:97
  814.1 36.4 %reduce-scatter.5.cloned.1.call-done = bf16[128,256]{1,0:T(8,128)(2,1)} async-done(((bf16[512,256]{1,0:T(8,128)(2,1)}), bf16[128,256]{1,0:T(8,128)(2,1)}) %reduce-scatter.5.cloned.1.call-update) | async-done | bytes 65552 | tf_op jit(solution)/shard_map/reduce_scatter | solution.py:103
  854.0 144.5 %all-reduce.7.cloned.1.call-done = f32[256,256]{1,0:T(8,128)} async-done(((f32[256,256]{1,0:T(8,128)}), f32[256,256]{1,0:T(8,128)}) %all-reduce.7.cloned.1.call-update) | async-done | bytes 262160 | tf_op jit(solution)/shard_map/psum | solution.py:120
  (150 shorter events, 135.4 us)
Async XLA Ops:
  7.2 149.9 %all-reduce.9.cloned.1.call-start = ((), (), s32[]{:S(2)}) async-start(), calls=%async_computation.6 | async-start | bytes 262144 | tf_op jit(solution)/shard_map/psum | solution.py:47
  12.8 590.1 %all-reduce.5.cloned.1.call-start = ((), (), s32[]{:S(2)}) async-start(), calls=%async_computation.2 | async-start | bytes 524288 | tf_op jit(solution)/shard_map/psum | solution.py:77
  162.9 12.4 %collective-permute-start = (bf16[4,128,256]{2,1,0:T(8,128)(2,1)S(1)}, bf16[4,128,256]{2,1,0:T(8,128)(2,1)S(1)}, u32[]{:S(2)}, u32[]{:S(2)}) collective-permute-start(bf16[4,128,256]{2,1,0:T(8,128)(2,1)S(1)} %copy.30), channel_id=1, source_target_pairs={{0,4},{4,8},{8,12},{12,16},{16,20},{20,24},{24,28},{28,32},{32,36}... | collective-permute-start | bytes 786440 | tf_op jit(solution)/shard_map/while/body/eval_jaxpr/ppermute | solution.py:9
  175.3 11.5 %collective-permute-start = (bf16[4,128,256]{2,1,0:T(8,128)(2,1)S(1)}, bf16[4,128,256]{2,1,0:T(8,128)(2,1)S(1)}, u32[]{:S(2)}, u32[]{:S(2)}) collective-permute-start(bf16[4,128,256]{2,1,0:T(8,128)(2,1)S(1)} %copy.30), channel_id=1, source_target_pairs={{0,4},{4,8},{8,12},{12,16},{16,20},{20,24},{24,28},{28,32},{32,36}... | collective-permute-start | bytes 786440 | tf_op jit(solution)/shard_map/while/body/eval_jaxpr/ppermute | solution.py:9
  186.8 11.0 %collective-permute-start = (bf16[4,128,256]{2,1,0:T(8,128)(2,1)S(1)}, bf16[4,128,256]{2,1,0:T(8,128)(2,1)S(1)}, u32[]{:S(2)}, u32[]{:S(2)}) collective-permute-start(bf16[4,128,256]{2,1,0:T(8,128)(2,1)S(1)} %copy.30), channel_id=1, source_target_pairs={{0,4},{4,8},{8,12},{12,16},{16,20},{20,24},{24,28},{28,32},{32,36}... | collective-permute-start | bytes 786440 | tf_op jit(solution)/shard_map/while/body/eval_jaxpr/ppermute | solution.py:9
  197.9 11.0 %collective-permute-start = (bf16[4,128,256]{2,1,0:T(8,128)(2,1)S(1)}, bf16[4,128,256]{2,1,0:T(8,128)(2,1)S(1)}, u32[]{:S(2)}, u32[]{:S(2)}) collective-permute-start(bf16[4,128,256]{2,1,0:T(8,128)(2,1)S(1)} %copy.30), channel_id=1, source_target_pairs={{0,4},{4,8},{8,12},{12,16},{16,20},{20,24},{24,28},{28,32},{32,36}... | collective-permute-start | bytes 786440 | tf_op jit(solution)/shard_map/while/body/eval_jaxpr/ppermute | solution.py:9
  208.9 11.0 %collective-permute-start = (bf16[4,128,256]{2,1,0:T(8,128)(2,1)S(1)}, bf16[4,128,256]{2,1,0:T(8,128)(2,1)S(1)}, u32[]{:S(2)}, u32[]{:S(2)}) collective-permute-start(bf16[4,128,256]{2,1,0:T(8,128)(2,1)S(1)} %copy.30), channel_id=1, source_target_pairs={{0,4},{4,8},{8,12},{12,16},{16,20},{20,24},{24,28},{28,32},{32,36}... | collective-permute-start | bytes 786440 | tf_op jit(solution)/shard_map/while/body/eval_jaxpr/ppermute | solution.py:9
  219.9 11.0 %collective-permute-start = (bf16[4,128,256]{2,1,0:T(8,128)(2,1)S(1)}, bf16[4,128,256]{2,1,0:T(8,128)(2,1)S(1)}, u32[]{:S(2)}, u32[]{:S(2)}) collective-permute-start(bf16[4,128,256]{2,1,0:T(8,128)(2,1)S(1)} %copy.30), channel_id=1, source_target_pairs={{0,4},{4,8},{8,12},{12,16},{16,20},{20,24},{24,28},{28,32},{32,36}... | collective-permute-start | bytes 786440 | tf_op jit(solution)/shard_map/while/body/eval_jaxpr/ppermute | solution.py:9
  231.0 11.0 %collective-permute-start = (bf16[4,128,256]{2,1,0:T(8,128)(2,1)S(1)}, bf16[4,128,256]{2,1,0:T(8,128)(2,1)S(1)}, u32[]{:S(2)}, u32[]{:S(2)}) collective-permute-start(bf16[4,128,256]{2,1,0:T(8,128)(2,1)S(1)} %copy.30), channel_id=1, source_target_pairs={{0,4},{4,8},{8,12},{12,16},{16,20},{20,24},{24,28},{28,32},{32,36}... | collective-permute-start | bytes 786440 | tf_op jit(solution)/shard_map/while/body/eval_jaxpr/ppermute | solution.py:9
  242.0 11.0 %collective-permute-start = (bf16[4,128,256]{2,1,0:T(8,128)(2,1)S(1)}, bf16[4,128,256]{2,1,0:T(8,128)(2,1)S(1)}, u32[]{:S(2)}, u32[]{:S(2)}) collective-permute-start(bf16[4,128,256]{2,1,0:T(8,128)(2,1)S(1)} %copy.30), channel_id=1, source_target_pairs={{0,4},{4,8},{8,12},{12,16},{16,20},{20,24},{24,28},{28,32},{32,36}... | collective-permute-start | bytes 786440 | tf_op jit(solution)/shard_map/while/body/eval_jaxpr/ppermute | solution.py:9
  253.0 12.0 %collective-permute-start = (bf16[4,128,256]{2,1,0:T(8,128)(2,1)S(1)}, bf16[4,128,256]{2,1,0:T(8,128)(2,1)S(1)}, u32[]{:S(2)}, u32[]{:S(2)}) collective-permute-start(bf16[4,128,256]{2,1,0:T(8,128)(2,1)S(1)} %copy.30), channel_id=1, source_target_pairs={{0,4},{4,8},{8,12},{12,16},{16,20},{20,24},{24,28},{28,32},{32,36}... | collective-permute-start | bytes 786440 | tf_op jit(solution)/shard_map/while/body/eval_jaxpr/ppermute | solution.py:9
  265.1 13.1 %collective-permute-start = (bf16[4,128,256]{2,1,0:T(8,128)(2,1)S(1)}, bf16[4,128,256]{2,1,0:T(8,128)(2,1)S(1)}, u32[]{:S(2)}, u32[]{:S(2)}) collective-permute-start(bf16[4,128,256]{2,1,0:T(8,128)(2,1)S(1)} %copy.30), channel_id=1, source_target_pairs={{0,4},{4,8},{8,12},{12,16},{16,20},{20,24},{24,28},{28,32},{32,36}... | collective-permute-start | bytes 786440 | tf_op jit(solution)/shard_map/while/body/eval_jaxpr/ppermute | solution.py:9
  278.3 13.7 %collective-permute-start = (bf16[4,128,256]{2,1,0:T(8,128)(2,1)S(1)}, bf16[4,128,256]{2,1,0:T(8,128)(2,1)S(1)}, u32[]{:S(2)}, u32[]{:S(2)}) collective-permute-start(bf16[4,128,256]{2,1,0:T(8,128)(2,1)S(1)} %copy.30), channel_id=1, source_target_pairs={{0,4},{4,8},{8,12},{12,16},{16,20},{20,24},{24,28},{28,32},{32,36}... | collective-permute-start | bytes 786440 | tf_op jit(solution)/shard_map/while/body/eval_jaxpr/ppermute | solution.py:9
  292.0 12.8 %collective-permute-start = (bf16[4,128,256]{2,1,0:T(8,128)(2,1)S(1)}, bf16[4,128,256]{2,1,0:T(8,128)(2,1)S(1)}, u32[]{:S(2)}, u32[]{:S(2)}) collective-permute-start(bf16[4,128,256]{2,1,0:T(8,128)(2,1)S(1)} %copy.30), channel_id=1, source_target_pairs={{0,4},{4,8},{8,12},{12,16},{16,20},{20,24},{24,28},{28,32},{32,36}... | collective-permute-start | bytes 786440 | tf_op jit(solution)/shard_map/while/body/eval_jaxpr/ppermute | solution.py:9
  304.8 11.9 %collective-permute-start = (bf16[4,128,256]{2,1,0:T(8,128)(2,1)S(1)}, bf16[4,128,256]{2,1,0:T(8,128)(2,1)S(1)}, u32[]{:S(2)}, u32[]{:S(2)}) collective-permute-start(bf16[4,128,256]{2,1,0:T(8,128)(2,1)S(1)} %copy.30), channel_id=1, source_target_pairs={{0,4},{4,8},{8,12},{12,16},{16,20},{20,24},{24,28},{28,32},{32,36}... | collective-permute-start | bytes 786440 | tf_op jit(solution)/shard_map/while/body/eval_jaxpr/ppermute | solution.py:9
  316.7 11.0 %collective-permute-start = (bf16[4,128,256]{2,1,0:T(8,128)(2,1)S(1)}, bf16[4,128,256]{2,1,0:T(8,128)(2,1)S(1)}, u32[]{:S(2)}, u32[]{:S(2)}) collective-permute-start(bf16[4,128,256]{2,1,0:T(8,128)(2,1)S(1)} %copy.30), channel_id=1, source_target_pairs={{0,4},{4,8},{8,12},{12,16},{16,20},{20,24},{24,28},{28,32},{32,36}... | collective-permute-start | bytes 786440 | tf_op jit(solution)/shard_map/while/body/eval_jaxpr/ppermute | solution.py:9
  327.7 11.0 %collective-permute-start = (bf16[4,128,256]{2,1,0:T(8,128)(2,1)S(1)}, bf16[4,128,256]{2,1,0:T(8,128)(2,1)S(1)}, u32[]{:S(2)}, u32[]{:S(2)}) collective-permute-start(bf16[4,128,256]{2,1,0:T(8,128)(2,1)S(1)} %copy.30), channel_id=1, source_target_pairs={{0,4},{4,8},{8,12},{12,16},{16,20},{20,24},{24,28},{28,32},{32,36}... | collective-permute-start | bytes 786440 | tf_op jit(solution)/shard_map/while/body/eval_jaxpr/ppermute | solution.py:9
  338.8 11.0 %collective-permute-start = (bf16[4,128,256]{2,1,0:T(8,128)(2,1)S(1)}, bf16[4,128,256]{2,1,0:T(8,128)(2,1)S(1)}, u32[]{:S(2)}, u32[]{:S(2)}) collective-permute-start(bf16[4,128,256]{2,1,0:T(8,128)(2,1)S(1)} %copy.30), channel_id=1, source_target_pairs={{0,4},{4,8},{8,12},{12,16},{16,20},{20,24},{24,28},{28,32},{32,36}... | collective-permute-start | bytes 786440 | tf_op jit(solution)/shard_map/while/body/eval_jaxpr/ppermute | solution.py:9
  349.8 11.0 %collective-permute-start = (bf16[4,128,256]{2,1,0:T(8,128)(2,1)S(1)}, bf16[4,128,256]{2,1,0:T(8,128)(2,1)S(1)}, u32[]{:S(2)}, u32[]{:S(2)}) collective-permute-start(bf16[4,128,256]{2,1,0:T(8,128)(2,1)S(1)} %copy.30), channel_id=1, source_target_pairs={{0,4},{4,8},{8,12},{12,16},{16,20},{20,24},{24,28},{28,32},{32,36}... | collective-permute-start | bytes 786440 | tf_op jit(solution)/shard_map/while/body/eval_jaxpr/ppermute | solution.py:9
  360.8 11.0 %collective-permute-start = (bf16[4,128,256]{2,1,0:T(8,128)(2,1)S(1)}, bf16[4,128,256]{2,1,0:T(8,128)(2,1)S(1)}, u32[]{:S(2)}, u32[]{:S(2)}) collective-permute-start(bf16[4,128,256]{2,1,0:T(8,128)(2,1)S(1)} %copy.30), channel_id=1, source_target_pairs={{0,4},{4,8},{8,12},{12,16},{16,20},{20,24},{24,28},{28,32},{32,36}... | collective-permute-start | bytes 786440 | tf_op jit(solution)/shard_map/while/body/eval_jaxpr/ppermute | solution.py:9
  371.9 11.0 %collective-permute-start = (bf16[4,128,256]{2,1,0:T(8,128)(2,1)S(1)}, bf16[4,128,256]{2,1,0:T(8,128)(2,1)S(1)}, u32[]{:S(2)}, u32[]{:S(2)}) collective-permute-start(bf16[4,128,256]{2,1,0:T(8,128)(2,1)S(1)} %copy.30), channel_id=1, source_target_pairs={{0,4},{4,8},{8,12},{12,16},{16,20},{20,24},{24,28},{28,32},{32,36}... | collective-permute-start | bytes 786440 | tf_op jit(solution)/shard_map/while/body/eval_jaxpr/ppermute | solution.py:9
  382.9 11.6 %collective-permute-start = (bf16[4,128,256]{2,1,0:T(8,128)(2,1)S(1)}, bf16[4,128,256]{2,1,0:T(8,128)(2,1)S(1)}, u32[]{:S(2)}, u32[]{:S(2)}) collective-permute-start(bf16[4,128,256]{2,1,0:T(8,128)(2,1)S(1)} %copy.30), channel_id=1, source_target_pairs={{0,4},{4,8},{8,12},{12,16},{16,20},{20,24},{24,28},{28,32},{32,36}... | collective-permute-start | bytes 786440 | tf_op jit(solution)/shard_map/while/body/eval_jaxpr/ppermute | solution.py:9
  394.6 12.7 %collective-permute-start = (bf16[4,128,256]{2,1,0:T(8,128)(2,1)S(1)}, bf16[4,128,256]{2,1,0:T(8,128)(2,1)S(1)}, u32[]{:S(2)}, u32[]{:S(2)}) collective-permute-start(bf16[4,128,256]{2,1,0:T(8,128)(2,1)S(1)} %copy.30), channel_id=1, source_target_pairs={{0,4},{4,8},{8,12},{12,16},{16,20},{20,24},{24,28},{28,32},{32,36}... | collective-permute-start | bytes 786440 | tf_op jit(solution)/shard_map/while/body/eval_jaxpr/ppermute | solution.py:9
  407.3 14.1 %collective-permute-start = (bf16[4,128,256]{2,1,0:T(8,128)(2,1)S(1)}, bf16[4,128,256]{2,1,0:T(8,128)(2,1)S(1)}, u32[]{:S(2)}, u32[]{:S(2)}) collective-permute-start(bf16[4,128,256]{2,1,0:T(8,128)(2,1)S(1)} %copy.30), channel_id=1, source_target_pairs={{0,4},{4,8},{8,12},{12,16},{16,20},{20,24},{24,28},{28,32},{32,36}... | collective-permute-start | bytes 786440 | tf_op jit(solution)/shard_map/while/body/eval_jaxpr/ppermute | solution.py:9
  421.4 13.3 %collective-permute-start = (bf16[4,128,256]{2,1,0:T(8,128)(2,1)S(1)}, bf16[4,128,256]{2,1,0:T(8,128)(2,1)S(1)}, u32[]{:S(2)}, u32[]{:S(2)}) collective-permute-start(bf16[4,128,256]{2,1,0:T(8,128)(2,1)S(1)} %copy.30), channel_id=1, source_target_pairs={{0,4},{4,8},{8,12},{12,16},{16,20},{20,24},{24,28},{28,32},{32,36}... | collective-permute-start | bytes 786440 | tf_op jit(solution)/shard_map/while/body/eval_jaxpr/ppermute | solution.py:9
  434.7 12.3 %collective-permute-start = (bf16[4,128,256]{2,1,0:T(8,128)(2,1)S(1)}, bf16[4,128,256]{2,1,0:T(8,128)(2,1)S(1)}, u32[]{:S(2)}, u32[]{:S(2)}) collective-permute-start(bf16[4,128,256]{2,1,0:T(8,128)(2,1)S(1)} %copy.30), channel_id=1, source_target_pairs={{0,4},{4,8},{8,12},{12,16},{16,20},{20,24},{24,28},{28,32},{32,36}... | collective-permute-start | bytes 786440 | tf_op jit(solution)/shard_map/while/body/eval_jaxpr/ppermute | solution.py:9
  447.1 11.4 %collective-permute-start = (bf16[4,128,256]{2,1,0:T(8,128)(2,1)S(1)}, bf16[4,128,256]{2,1,0:T(8,128)(2,1)S(1)}, u32[]{:S(2)}, u32[]{:S(2)}) collective-permute-start(bf16[4,128,256]{2,1,0:T(8,128)(2,1)S(1)} %copy.30), channel_id=1, source_target_pairs={{0,4},{4,8},{8,12},{12,16},{16,20},{20,24},{24,28},{28,32},{32,36}... | collective-permute-start | bytes 786440 | tf_op jit(solution)/shard_map/while/body/eval_jaxpr/ppermute | solution.py:9
  458.5 11.0 %collective-permute-start = (bf16[4,128,256]{2,1,0:T(8,128)(2,1)S(1)}, bf16[4,128,256]{2,1,0:T(8,128)(2,1)S(1)}, u32[]{:S(2)}, u32[]{:S(2)}) collective-permute-start(bf16[4,128,256]{2,1,0:T(8,128)(2,1)S(1)} %copy.30), channel_id=1, source_target_pairs={{0,4},{4,8},{8,12},{12,16},{16,20},{20,24},{24,28},{28,32},{32,36}... | collective-permute-start | bytes 786440 | tf_op jit(solution)/shard_map/while/body/eval_jaxpr/ppermute | solution.py:9
  491.6 11.0 %collective-permute-start = (bf16[4,128,256]{2,1,0:T(8,128)(2,1)S(1)}, bf16[4,128,256]{2,1,0:T(8,128)(2,1)S(1)}, u32[]{:S(2)}, u32[]{:S(2)}) collective-permute-start(bf16[4,128,256]{2,1,0:T(8,128)(2,1)S(1)} %copy.30), channel_id=1, source_target_pairs={{0,4},{4,8},{8,12},{12,16},{16,20},{20,24},{24,28},{28,32},{32,36}... | collective-permute-start | bytes 786440 | tf_op jit(solution)/shard_map/while/body/eval_jaxpr/ppermute | solution.py:9
  535.6 276.9 %reduce-scatter.3.cloned.1.call-start = ((), (), s32[]{:S(2)}) async-start(), calls=%async_computation.3 | async-start | bytes 8650752 | tf_op jit(solution)/shard_map/reduce_scatter | solution.py:97
  631.7 218.9 %reduce-scatter.5.cloned.1.call-start = ((), (), s32[]{:S(2)}) async-start(), calls=%async_computation.4 | async-start | bytes 327680 | tf_op jit(solution)/shard_map/reduce_scatter | solution.py:103
  812.4 186.1 %all-reduce.7.cloned.1.call-start = ((), (), s32[]{:S(2)}) async-start(), calls=%async_computation.5 | async-start | bytes 524288 | tf_op jit(solution)/shard_map/psum | solution.py:120
  (10 other events, 604.3 us)
Sparse Core Ops, SparseCore 0:
  13.5 143.5 all-reduce.8
  535.7 67.1 all-reduce.4
  631.8 180.6 reduce-scatter.2
  814.6 35.8 reduce-scatter.4
  856.4 142.0 all-reduce.6
where the time goes:
time: 1010 us
  waiting for transfers between devices  903 us (89%)
  local copies, waits for them, and re-layouts  51.6 us (5%)
  matrix products  23.8 us (2%)
  between operations  14.5 us (1%)
    ppermute x31, waiting for transfers between devices, from_behind(): lax.ppermute(shard, axis, [(i, (i + by) % devices) for i in range(devices)])  335 us
    reduce_scatter x1, waiting for transfers between devices, shards(): lax.psum_scatter(spread.reshape(row_count, feat_dim).astype(jnp.bfloat16)...  181 us
    psum x1, waiting for transfers between devices, shards(): weight_grad = lax.psum(weight_local, ('row', 'rep'))  144 us
    psum x1, waiting for transfers between devices, shards(): col_total, row_total = lax.psum((col_full, row_full), ('row', 'rep'))  140 us
    psum x1, waiting for transfers between devices, shards(): lax.psum(summed_local.astype(jnp.bfloat16), 'rep').astype(jnp.float32)  66.6 us
    reduce_scatter x1, waiting for transfers between devices, shards(): lax.psum_scatter(group_part, 'rep', scatter_dimension=0, tiled=True)  36.4 us
    dynamic_update_slice x31, local copies, waits for them, and re-layouts, every_section(): stack = lax.dynamic_update_index_in_dim(stack, held_panel, section_idx, 0)  22.5 us
  transfers between devices with their start and end apart: 36, of which 36 were waited for; matrix products, arithmetic and copies ran while one was open for 3% of the time, Pallas kernels for 0%

commit v1 on v0

v1 whole, which is shorter than its diff:
```python
import functools

import jax
import jax.numpy as jnp
from jax import lax
from jax.experimental import pallas as pl
from jax.experimental.pallas import tpu as pltpu
from jax.sharding import PartitionSpec as P

MESH = pl.DeviceIdType.MESH
BLK = 128
FEAT = 256
ROWS = 512
F32 = jnp.float32
BF16 = jnp.bfloat16


def keep_mask(node_ids, feat_ids, key0, key1):
    mixed = node_ids * 73856093 ^ feat_ids * 19349663 ^ key0 * 83492791 ^ key1
    mixed = mixed ^ lax.shift_right_logical(mixed, jnp.int32(13))
    mixed = mixed * 1274126177
    mixed = mixed ^ lax.shift_right_logical(mixed, jnp.int32(16))
    return mixed & 1023 < 819


def place(y, x, z, c):
    y, x, z = y % 4, x % 4, z % 4
    return ((y // 2) * 16 + x * 4 + z, (y % 2) * 2 + c)


def build_kernel(idx_ref, keep_ref, tiles_ref, d_ref, col_ref, row_ref):
    i = pl.program_id(0)

    @pl.when(i == 0)
    def _():
        col_ref[...] = jnp.zeros_like(col_ref)

    d_ref[...] = jnp.zeros_like(d_ref)
    row_acc = jnp.zeros((BLK, BLK), F32)
    for k in range(16):
        slot = idx_ref[i, k]
        tile = tiles_ref[0, k].astype(F32) * keep_ref[i, k].astype(F32)
        at = pl.ds(pl.multiple_of(slot * BLK, BLK), BLK)
        d_ref[:, at] = (d_ref[:, at].astype(F32) + tile).astype(BF16)
        col_ref[pl.ds(slot, 1), :] += jnp.sum(tile, axis=0, keepdims=True)
        row_acc = row_acc + tile
    row_ref[pl.ds(i, 1), :] = jnp.sum(row_acc.T, axis=0, keepdims=True)


def build(idx, keep, tiles):
    return pl.pallas_call(
        build_kernel,
        grid_spec=pltpu.PrefetchScalarGridSpec(
            num_scalar_prefetch=2,
            grid=(4,),
            in_specs=[pl.BlockSpec((1, 16, BLK, BLK), lambda i, a, b: (i, 0, 0, 0))],
            out_specs=[
                pl.BlockSpec((BLK, 32 * BLK), lambda i, a, b: (i, 0)),
                pl.BlockSpec((32, BLK), lambda i, a, b: (0, 0)),
                pl.BlockSpec((4, BLK), lambda i, a, b: (0, 0)),
            ],
        ),
        out_shape=[
            jax.ShapeDtypeStruct((ROWS, 32 * BLK), BF16),
            jax.ShapeDtypeStruct((32, BLK), F32),
            jax.ShapeDtypeStruct((4, BLK), F32),
        ],
        name="build",
    )(idx, keep, tiles)


def layer_kernel(
    key_ref, feat_hbm, w_hbm, d_hbm, col_ref, row_ref, cot_hbm,
    hid_hbm, wg_hbm, fg_hbm,
    feat, w, d, cot, own, xs, cols, scales, deg1, deg2, rdeg, hT, part, e1, e2s, e2r, tot,
    hid, pushed, pushT, tt, bx1, bx2, u, fin, g, w1, g1, w2, g2, w3, g3, g4, gout, fg,
    in_sem, out_sem, s1_s, s1_r, x_s, x_r, d1_s, d1_r, d2_s, d2_r, rd_s, rd_r,
    e_s, e_r, b_s, b_r, f_s, f_r, w1_s, w1_r, w2_s, w2_r, w3_s, w3_r, w4_s, w4_r, w5_s, w5_r,
):
    row = lax.axis_index("row")
    q = lax.axis_index("rep")
    y = (row // 16) * 2 + q // 2
    x = (row // 4) % 4
    z = row % 4
    c = q % 2
    yh = row // 16
    yl = q // 2
    zp = z + 4 - q
    me8 = yh * 4 + q
    sent = []

    def remote(src, dst, ssem, rsem, to):
        return pltpu.make_async_remote_copy(
            src_ref=src, dst_ref=dst, send_sem=ssem, recv_sem=rsem, device_id=to, device_id_type=MESH
        )

    def send(src, dst, ssem, rsem, to):
        copy = remote(src, dst, ssem, rsem, to)
        copy.start()
        sent.append(copy)
        return copy

    loads = [
        pltpu.make_async_copy(src, dst, in_sem.at[n])
        for n, (src, dst) in enumerate(((feat_hbm, feat), (d_hbm, d), (w_hbm, w), (cot_hbm, cot)))
    ]
    for copy in loads:
        copy.start()

    barrier = pltpu.get_barrier_semaphore()
    place32 = y * 8 + z * 2 + c
    for n in range(1, 32):
        other = (place32 + n) % 32
        pl.semaphore_signal(
            barrier, inc=1, device_id=place(other // 8, x, (other // 2) % 4, other % 2), device_id_type=MESH
        )
    for n in range(1, 4):
        pl.semaphore_signal(barrier, inc=1, device_id=place(y, x + n, z, c), device_id_type=MESH)

    loads[0].wait()
    key0, key1 = key_ref[0], key_ref[1]
    for i in range(4):
        nodes = row * ROWS + i * BLK + lax.broadcasted_iota(jnp.int32, (BLK, FEAT), 0)
        feats = lax.broadcasted_iota(jnp.int32, (BLK, FEAT), 1)
        at = pl.ds(i * BLK, BLK)
        kept = keep_mask(nodes, feats, key0, key1)
        own[at, :] = jnp.where(kept, feat[at, :].astype(F32), 0.0).astype(BF16)
    cols[...] = col_ref[...]
    pl.semaphore_wait(barrier, 34)

    d1 = [
        send(cols, deg1.at[n - 1], d1_s.at[n - 1], d1_r.at[n - 1], place(y, x + n, z, c))
        for n in range(1, 4)
    ]
    rdeg[0] = row_ref[...]
    rd = []
    for n in range(1, 4):
        other = (q + n) % 4
        rd.append(send(rdeg.at[0], rdeg.at[n], rd_s.at[n - 1], rd_r.at[n - 1], (row, other)))

    to_same = remote(own, xs.at[yh * 4 + x], s1_s.at[0], s1_r.at[0], place(y, x, z + q, c))
    q_flip = 2 * (1 - yl) + c

    @pl.when(q != 0)
    def _():
        to_same.start()

    flip = send(own, xs.at[yh * 4 + x], s1_s.at[1], s1_r.at[1], place(3 - y, x, z + q_flip, c))

    @pl.when(q == 0)
    def _():
        xs[yh * 4 + x] = own[...]

    @pl.when(q != 0)
    def _():
        to_same.wait_recv()

    right, left = place(y, x + 1, z, c), place(y, x + 3, z, c)

    def hop(panel, n, to):
        return send(xs.at[panel], xs.at[panel], x_s.at[n], x_r.at[n], to)

    same, other = yh * 4 + x, (1 - yh) * 4 + x
    xr, xl = (x + 1) % 4, (x + 3) % 4
    same_right = hop(same, 0, right)
    same_left = hop(same, 1, left)
    flip.wait_recv()
    other_right = hop(other, 2, right)
    other_left = hop(other, 3, left)

    for copy in d1:
        copy.wait_recv()
    colx = cols[...] + deg1[0] + deg1[1] + deg1[2]
    deg2[0] = colx
    d2 = []
    for n in range(1, 8):
        o = (me8 + n) % 8
        o_q = o % 4
        to = place((o // 4) * 2 + o_q // 2, x, zp + o_q, o_q % 2)
        d2.append(send(deg2.at[0], deg2.at[n], d2_s.at[n - 1], d2_r.at[n - 1], to))

    same_right.wait_recv()
    far_right = hop(yh * 4 + xl, 4, right)
    other_left.wait_recv()
    far_left = hop((1 - yh) * 4 + xr, 5, left)

    for copy in d2:
        copy.wait_recv()
    total = deg2[0]
    for n in range(1, 8):
        total = total + deg2[n]
    scales[...] = lax.rsqrt(1.0 + total)
    for copy in rd:
        copy.wait_recv()
    by_rep = [rdeg[(q + 4 - s) % 4] for s in range(4)]
    row_total = (by_rep[0] + by_rep[1]) + (by_rep[2] + by_rep[3])
    row_scale = lax.rsqrt(1.0 + row_total)
    row_cols = jnp.concatenate([row_scale, row_scale], axis=0).T

    loads[1].wait()
    eye = lax.broadcasted_iota(jnp.int32, (BLK, BLK), 0) == lax.broadcasted_iota(jnp.int32, (BLK, BLK), 1)
    eye = jnp.where(eye, 1.0, 0.0)
    for l in range(32):
        flag = jnp.where(jnp.logical_and(q == 0, yh * 4 + x == l // 4), 1.0, 0.0)
        scale = scales[pl.ds(l, 1), :]
        for i in range(4):
            block = d[pl.ds(i * BLK, BLK), pl.ds(l * BLK, BLK)].astype(F32)
            if i == l % 4:
                block = block + eye * flag
            d[pl.ds(i * BLK, BLK), pl.ds(l * BLK, BLK)] = (block * scale).astype(BF16)

    def panel_cols(p):
        return pl.ds(pl.multiple_of(p * ROWS, ROWS), ROWS)

    def term(p):
        return jnp.dot(d[:, panel_cols(p)], xs[p], preferred_element_type=F32)

    acc = term(same) + term(other)
    acc = acc + term(yh * 4 + xl)
    acc = acc + term((1 - yh) * 4 + xr)
    same_left.wait_recv()
    acc = acc + term(yh * 4 + xr)
    other_right.wait_recv()
    acc = acc + term((1 - yh) * 4 + xl)
    xo = (x + 2) % 4
    far_right.wait_recv()
    acc = acc + term(yh * 4 + xo)
    far_left.wait_recv()
    acc = acc + term((1 - yh) * 4 + xo)
    h = acc.astype(BF16)
    loads[2].wait()
    part[...] = (jnp.dot(h, w[...], preferred_element_type=F32) * 1.25).astype(BF16)

    half = ROWS // 2
    mine = pl.ds(pl.multiple_of(c * half, half), half)
    theirs = pl.ds(pl.multiple_of((1 - c) * half, half), half)
    partner = place(y, x, z, 1 - c)
    e1_copy = send(part.at[theirs], e1, e_s.at[0], e_r.at[0], partner)
    hT[...] = acc.T.astype(BF16)
    e1_copy.wait_recv()
    e2s[...] = (part[mine, :].astype(F32) + e1[...].astype(F32)).astype(BF16)
    e2_copy = send(e2s, e2r, e_s.at[1], e_r.at[1], (row, (1 - yl) * 2 + c))
    e2_copy.wait_recv()
    tot[mine, :] = (e2s[...].astype(F32) + e2r[...].astype(F32)).astype(BF16)
    e3_copy = send(tot.at[mine], tot.at[mine], e_s.at[2], e_r.at[2], partner)
    loads[3].wait()
    e3_copy.wait_recv()

    for i in range(4):
        at = pl.ds(i * BLK, BLK)
        r = row_cols[:, i : i + 1]
        pre = tot[at, :].astype(F32) * r
        s = 1.0 / (1.0 + jnp.exp(-pre))
        hid[at, :] = (pre * s).astype(BF16)
        grad = cot[at, :].astype(F32) * s * (1.0 + pre * (1.0 - s)) * r
        pushed[at, :] = grad.astype(BF16)
        pushT[:, at] = grad.T.astype(BF16)
    hid_out = pltpu.make_async_copy(hid, hid_hbm, out_sem.at[0])
    hid_out.start()

    def back(p):
        out = jnp.dot(pushT[...], d[:, panel_cols(p)], preferred_element_type=F32).astype(BF16)
        for j in range(4):
            tt[p, j] = out[:, j * BLK : (j + 1) * BLK]

    back(xo)
    far0 = send(tt.at[xo], bx1.at[0], b_s.at[0], b_r.at[0], right)
    back(4 + xo)
    far1 = send(tt.at[4 + xo], bx1.at[1], b_s.at[1], b_r.at[1], left)
    back(4 + xr)
    near1r = send(tt.at[4 + xr], bx2.at[1], b_s.at[2], b_r.at[2], right)
    back(xl)
    near0l = send(tt.at[xl], bx2.at[2], b_s.at[3], b_r.at[3], left)
    back(xr)
    back(4 + xl)
    g[...] = jnp.dot(hT[...], pushed[...], preferred_element_type=F32) * 1.25
    wx = []
    for n in range(1, 4):
        xt = (x + n) % 4
        rows = pl.ds(pl.multiple_of(xt * 64, 64), 64)
        wx.append(send(g.at[rows], w1.at[n - 1], w1_s.at[n - 1], w1_r.at[n - 1], place(y, xt, z, c)))
    far0.wait_recv()
    tt[xr] = (tt[xr].astype(F32) + bx1[0].astype(F32)).astype(BF16)
    near0r = send(tt.at[xr], bx2.at[0], b_s.at[4], b_r.at[4], right)
    far1.wait_recv()
    tt[4 + xl] = (tt[4 + xl].astype(F32) + bx1[1].astype(F32)).astype(BF16)
    near1l = send(tt.at[4 + xl], bx2.at[3], b_s.at[5], b_r.at[5], left)
    back(x)
    back(4 + x)

    place8 = y * 2 + c
    for copy in wx:
        copy.wait_recv()
    rows = pl.ds(pl.multiple_of(x * 64, 64), 64)
    g1[...] = g[rows, :] + w1[0] + w1[1] + w1[2]
    w2c = []
    for n in range(1, 8):
        o = (place8 + n) % 8
        src = g1.at[pl.ds(pl.multiple_of(o * 8, 8), 8)]
        w2c.append(send(src, w2.at[n - 1], w2_s.at[n - 1], w2_r.at[n - 1], place(o // 2, x, z, o % 2)))

    near0l.wait_recv()
    near0r.wait_recv()
    near1r.wait_recv()
    near1l.wait_recv()
    fins = []
    for h2 in range(2):
        p = h2 * 4 + x
        left_in, right_in = (bx2[0], bx2[2]) if h2 == 0 else (bx2[1], bx2[3])
        u[h2] = (tt[p].astype(F32) + left_in.astype(F32) + right_in.astype(F32)).astype(BF16)
        for j in range(4):
            n = h2 * 4 + j
            copy = remote(
                u.at[h2, j], fin.at[me8], f_s.at[n], f_r.at[me8], place(2 * h2 + j // 2, x, zp, j % 2)
            )
            if j == 0:
                is_self = jnp.logical_and(q == 0, yh == h2)

                @pl.when(jnp.logical_not(is_self))
                def _():
                    copy.start()

                @pl.when(is_self)
                def _():
                    fin[me8] = u[h2, 0]
            else:
                copy.start()
            fins.append(copy)

    for copy in w2c:
        copy.wait_recv()
    g2v = g1[pl.ds(pl.multiple_of(place8 * 8, 8), 8), :]
    for n in range(7):
        g2v = g2v + w2[n]
    g2[...] = g2v
    w3[z] = g2v
    w3c = []
    for n in range(1, 4):
        w3c.append(send(g2, w3.at[z], w3_s.at[n - 1], w3_r.at[n - 1], place(y, x, z + n, c)))
    for copy in w3c:
        copy.wait_recv()
    g4_at = pl.ds(pl.multiple_of(place8 * 8, 8), 8)
    g4[g4_at, :] = (w3[0] + w3[1]) + (w3[2] + w3[3])
    w4c = []
    for n in range(1, 8):
        o = (place8 + n) % 8
        w4c.append(
            send(g4.at[g4_at], g4.at[g4_at], w4_s.at[n - 1], w4_r.at[n - 1], place(o // 2, x, z, o % 2))
        )
    for copy in w4c:
        copy.wait_recv()
    gout[rows, :] = g4[...]
    w5c = []
    for n in range(1, 4):
        w5c.append(send(g4, gout.at[rows], w5_s.at[n - 1], w5_r.at[n - 1], place(y, x + n, z, c)))

    for n in range(8):
        copy = remote(u.at[0, 0], fin.at[n], f_s.at[n], f_r.at[n], (row, q))
        if n % 4 == 0:

            @pl.when(jnp.logical_not(jnp.logical_and(q == 0, yh == n // 4)))
            def _():
                copy.wait_recv()
        else:
            copy.wait_recv()
    proj = fin[0].astype(F32)
    for n in range(1, 8):
        proj = proj + fin[n].astype(F32)
    proj = proj.T.astype(BF16)
    back_proj = lax.dot_general(proj, w[...], (((1,), (1,)), ((), ())), preferred_element_type=F32) * 1.25
    nodes = row * ROWS + q * BLK + lax.broadcasted_iota(jnp.int32, (BLK, FEAT), 0)
    feats = lax.broadcasted_iota(jnp.int32, (BLK, FEAT), 1)
    fg[...] = jnp.where(keep_mask(nodes, feats, key0, key1), back_proj, 0.0).astype(BF16)
    fg_out = pltpu.make_async_copy(fg, fg_hbm, out_sem.at[1])
    fg_out.start()
    for copy in w5c:
        copy.wait_recv()
    wg_out = pltpu.make_async_copy(gout, wg_hbm, out_sem.at[2])
    wg_out.start()

    @pl.when(q != 0)
    def _():
        to_same.wait_send()

    for copy in sent:
        copy.wait_send()
    for n, copy in enumerate(fins):
        if n % 4 == 0:

            @pl.when(jnp.logical_not(jnp.logical_and(q == 0, yh == n // 4)))
            def _():
                copy.wait_send()
        else:
            copy.wait_send()
    hid_out.wait()
    fg_out.wait()
    wg_out.wait()


def layer(drop_key, features, weight, d, col, row, cotangent):
    dma = pltpu.SemaphoreType.DMA
    vmem = pltpu.VMEM
    any_spec = pl.BlockSpec(memory_space=pl.ANY)
    vmem_spec = pl.BlockSpec(memory_space=pltpu.VMEM)
    return pl.pallas_call(
        layer_kernel,
        out_shape=[
            jax.ShapeDtypeStruct((ROWS, FEAT), BF16),
            jax.ShapeDtypeStruct((FEAT, FEAT), F32),
            jax.ShapeDtypeStruct((BLK, FEAT), BF16),
        ],
        in_specs=[
            pl.BlockSpec(memory_space=pltpu.SMEM),
            any_spec, any_spec, any_spec, vmem_spec, vmem_spec, any_spec,
        ],
        out_specs=[any_spec, any_spec, any_spec],
        scratch_shapes=[
            vmem((ROWS, FEAT), BF16),
            vmem((FEAT, FEAT), BF16),
            vmem((ROWS, 32 * BLK), BF16),
            vmem((ROWS, FEAT), BF16),
            vmem((ROWS, FEAT), BF16),
            vmem((8, ROWS, FEAT), BF16),
            vmem((32, BLK), F32),
            vmem((32, BLK), F32),
            vmem((3, 32, BLK), F32),
            vmem((8, 32, BLK), F32),
            vmem((4, 4, BLK), F32),
            vmem((FEAT, ROWS), BF16),
            vmem((ROWS, FEAT), BF16),
            vmem((ROWS // 2, FEAT), BF16),
            vmem((ROWS // 2, FEAT), BF16),
            vmem((ROWS // 2, FEAT), BF16),
            vmem((ROWS, FEAT), BF16),
            vmem((ROWS, FEAT), BF16),
            vmem((ROWS, FEAT), BF16),
            vmem((FEAT, ROWS), BF16),
            vmem((8, 4, FEAT, BLK), BF16),
            vmem((2, 4, FEAT, BLK), BF16),
            vmem((4, 4, FEAT, BLK), BF16),
            vmem((2, 4, FEAT, BLK), BF16),
            vmem((8, FEAT, BLK), BF16),
            vmem((FEAT, FEAT), F32),
            vmem((3, 64, FEAT), F32),
            vmem((64, FEAT), F32),
            vmem((7, 8, FEAT), F32),
            vmem((8, FEAT), F32),
            vmem((4, 8, FEAT), F32),
            vmem((8, FEAT), F32),
            vmem((64, FEAT), F32),
            vmem((FEAT, FEAT), F32),
            vmem((BLK, FEAT), BF16),
            dma((4,)), dma((3,)), dma((2,)), dma((2,)), dma((6,)), dma((6,)),
            dma((3,)), dma((3,)), dma((7,)), dma((7,)), dma((3,)), dma((3,)),
            dma((3,)), dma((3,)), dma((6,)), dma((6,)), dma((8,)), dma((8,)),
            dma((3,)), dma((3,)), dma((7,)), dma((7,)), dma((3,)), dma((3,)),
            dma((7,)), dma((7,)), dma((3,)), dma((3,)),
        ],
        compiler_params=pltpu.CompilerParams(
            collective_id=0, has_side_effects=True, vmem_limit_bytes=48 << 20
        ),
        name="layer",
    )(drop_key, features, weight, d, col, row, cotangent)


def shards(features, weight, adj_tiles, block_cols, edge_keep, drop_key, cotangent):
    idx = (block_cols // 16) * 4 + block_cols % 4
    d, col, row = build(idx, edge_keep, adj_tiles)
    hidden, weight_grad, feature_grad = layer(drop_key, features, weight, d, col, row, cotangent)
    return (hidden, weight_grad, feature_grad)


def solution(mesh):
    in_specs = (
        P("row", None),
        P(),
        P("row", "rep", None, None),
        P("row", "rep"),
        P("row", "rep"),
        P(),
        P("row", None),
    )
    out_specs = (P("row", None), P(), P(("row", "rep"), None))
    return jax.shard_map(shards, mesh=mesh, in_specs=in_specs, out_specs=out_specs, check_vma=False)
```

time: 1010 us -> 105 us (0.10)
  waiting for transfers between devices: 903 us -> 0 us
  Pallas kernels: 0 us -> 93.7 us
  local copies, waits for them, and re-layouts: 51.6 us -> 9.08 us
  matrix products: 23.8 us -> 0 us
  between operations: 14.5 us -> 0.65 us
    psum x3 -> x0, waiting for transfers between devices: 351 us -> none  [the longest x1 144 us: shards(): weight_grad = lax.psum(weight_local, ('row', 'rep'))]
    ppermute x31 -> x0, waiting for transfers between devices: 335 us -> none  [from_behind(): lax.ppermute(shard, axis, [(i, (i + by) % devices) for i in range(devices)])]
    reduce_scatter x2 -> x0, waiting for transfers between devices: 217 us -> none  [the longest x1 181 us: shards(): lax.psum_scatter(spread.reshape(row_count, feat_dim).astype(jnp.bfloat16)...]
    pallas_call x0 -> x2, Pallas kernels: none -> 93.7 us  [the longest x1 88.1 us: layer(): pl.pallas_call(layer_kernel, out_shape=[jax.ShapeDtypeStruct((ROWS, FEAT)...]
    dot_general x7 -> x0, matrix products: 23.8 us -> none  [the longest x1 13.4 us: shards(): jnp.einsum('sn,sbf->nbf', onehot, contribution, precision=lax.Precision.H...]
    dynamic_update_slice x33 -> x0, local copies, waits for them, and re-layouts: 23.3 us -> none  [the longest x31 22.5 us: every_section(): stack = lax.dynamic_update_index_in_dim(stack, held_panel, section_idx, 0)]
    convert_element_type x1 -> x0, local copies, waits for them, and re-layouts: 11.4 us -> none  [shards(): spread.reshape(row_count, feat_dim).astype(jnp.bfloat16)]
  transfers between devices with their start and end apart: 36 -> 0, of which waited for: 36 -> 0; matrix products, arithmetic and copies ran while one was open for 3% -> 0% of each run, Pallas kernels for 0% -> 0%
where the time goes in v1:
time: 105 us
  Pallas kernels  93.7 us (89%)
  local copies, waits for them, and re-layouts  9.08 us (9%)
  other arithmetic  1.27 us (1%)
    pallas_call x1, Pallas kernels, layer(): pl.pallas_call(layer_kernel, out_shape=[jax.ShapeDtypeStruct((ROWS, FEAT)...  88.1 us
    unnamed x17, local copies, waits for them, and re-layouts  9.08 us
    pallas_call x1, Pallas kernels, build(): pl.pallas_call(build_kernel, grid_spec=pltpu.PrefetchScalarGridSpec(num_s...  5.53 us

profile of v1, /device:TPU:1, one launch (start us, length us, event | category | flops | bytes accessed | tf_op | source)
XLA Modules:
  0.0 104.7 jit_solution(17703035126545367768)
XLA Ops:
  0.6 1.3 %fusion.2.idx_ref = s32[4,16]{1,0:T(4,128)} fusion(s32[4,16]{1,0:T(4,128)} %param.10), kind=kLoop, calls=%fused_computation.8 | loop fusion | flops 1600 | bytes 512 | tf_op jit(solution)/shard_map/add | solution.py:467
  1.9 5.5 %build.1 = (bf16[512,4096]{1,0:T(8,128)(2,1)}, f32[32,128]{1,0:T(8,128)}, f32[4,128]{1,0:T(4,128)}) custom-call(s32[4,16]{1,0:T(4,128)} %fusion.2.idx_ref, s32[4,16]{1,0:T(4,128)} %keep_ref.1, bf16[4,16,128,128]{3,2,1,0:T(8,128)(2,1)} %tiles_ref.1), custom_call_target="tpu_custom_call" | custom-call | tf_op jit(solution)/shard_map/build/pallas_call | solution.py:51
  7.4 0.0 copy-start
  7.4 2.2 %copy-done = bf16[512,4096]{1,0:T(8,128)(2,1)S(1)} copy-done((bf16[512,4096]{1,0:T(8,128)(2,1)S(1)}, bf16[512,4096]{1,0:T(8,128)(2,1)}, u32[]{:S(2)}) %copy-start) | copy-done | bytes 4194328
  9.6 0.0 copy-start.1
  9.6 0.9 copy-done.1
  10.6 0.0 copy-start.2
  10.6 0.9 copy-done.2
  11.5 0.0 copy-start.3
  11.5 0.9 copy-done.3
  12.4 0.0 copy-start.4
  12.4 0.7 copy-done.4
  13.1 0.0 copy-start.5
  13.1 0.7 copy-done.5
  13.8 0.0 copy-start.6
  13.8 0.7 copy-done.6
  14.5 88.1 %layer.1 = (bf16[512,256]{1,0:T(8,128)(2,1)S(1)}, f32[256,256]{1,0:T(8,128)S(1)}, bf16[128,256]{1,0:T(8,128)(2,1)S(1)}) custom-call(s32[2]{0:T(128)S(1)} %copy-done.6, bf16[512,256]{1,0:T(8,128)(2,1)S(1)} %copy-done.1, bf16[256,256]{1,0:T(8,128)(2,1)S(1)} %copy-done.3, bf16[512,4096]{1,0:T(8,128)(2,1)S(1)} %copy-done, f32[32,128]{1,0:T(8,128)S(1)} %copy-done.4, ...), custom_call_target="tpu_custom_call" | custom-call | tf_op jit(solution)/shard_map/layer/pallas_call | solution.py:405
  102.6 0.7 copy.13
  103.3 0.7 copy.14
  104.0 0.6 copy.15
Async XLA Ops:
  7.4 2.2 %copy-start = (bf16[512,4096]{1,0:T(8,128)(2,1)S(1)}, bf16[512,4096]{1,0:T(8,128)(2,1)}, u32[]{:S(2)}) copy-start(bf16[512,4096]{1,0:T(8,128)(2,1)} %get-tuple-element.6.d_hbm) | copy-start | bytes 12582916
  9.6 0.9 copy-start.1
  10.6 0.9 copy-start.2
  11.5 0.9 copy-start.3
  12.4 0.7 copy-start.4
  13.1 0.7 copy-start.5
  13.8 0.7 copy-start.6

commit v2 on v1

v2 whole, which is shorter than its diff:
```python
import functools

import jax
import jax.numpy as jnp
from jax import lax
from jax.experimental import pallas as pl
from jax.experimental.pallas import tpu as pltpu
from jax.sharding import PartitionSpec as P

MESH = pl.DeviceIdType.MESH
BLK = 128
FEAT = 256
ROWS = 512
CHUNKS = 4
F32 = jnp.float32
BF16 = jnp.bfloat16


def keep_mask(node_ids, feat_ids, key0, key1):
    mixed = node_ids * 73856093 ^ feat_ids * 19349663 ^ key0 * 83492791 ^ key1
    mixed = mixed ^ lax.shift_right_logical(mixed, jnp.int32(13))
    mixed = mixed * 1274126177
    mixed = mixed ^ lax.shift_right_logical(mixed, jnp.int32(16))
    return mixed & 1023 < 819


def place(y, x, z, c):
    y, x, z = y % 4, x % 4, z % 4
    return ((y // 2) * 16 + x * 4 + z, (y % 2) * 2 + c)


def build_kernel(blk_ref, keep_ref, tiles_ref, d_ref, col_ref, row_ref):
    i = pl.program_id(0)

    @pl.when(i == 0)
    def _():
        col_ref[...] = jnp.zeros_like(col_ref)

    d_ref[...] = jnp.zeros_like(d_ref)
    row_acc = jnp.zeros((BLK, BLK), F32)
    for k in range(16):
        col = blk_ref[i, k]
        slot = (col >> 4) * 4 + (col & 3)
        tile = tiles_ref[0, k].astype(F32) * keep_ref[i, k].astype(F32)
        at = pl.ds(pl.multiple_of(slot * BLK, BLK), BLK)
        d_ref[:, at] = (d_ref[:, at].astype(F32) + tile).astype(BF16)
        col_ref[pl.ds(slot, 1), :] += jnp.sum(tile, axis=0, keepdims=True)
        row_acc = row_acc + tile
    row_ref[pl.ds(i, 1), :] = jnp.sum(row_acc.T, axis=0, keepdims=True)


def build(cols, keep, tiles):
    return pl.pallas_call(
        build_kernel,
        grid_spec=pltpu.PrefetchScalarGridSpec(
            num_scalar_prefetch=2,
            grid=(4,),
            in_specs=[pl.BlockSpec((1, 16, BLK, BLK), lambda i, a, b: (i, 0, 0, 0))],
            out_specs=[
                pl.BlockSpec((BLK, 32 * BLK), lambda i, a, b: (i, 0)),
                pl.BlockSpec((32, BLK), lambda i, a, b: (0, 0)),
                pl.BlockSpec((4, BLK), lambda i, a, b: (0, 0)),
            ],
        ),
        out_shape=[
            jax.ShapeDtypeStruct((ROWS, 32 * BLK), BF16),
            jax.ShapeDtypeStruct((32, BLK), F32),
            jax.ShapeDtypeStruct((4, BLK), F32),
        ],
        name="build",
    )(cols, keep, tiles)


def layer_kernel(
    key_ref, feat_hbm, w_hbm, d_hbm, col_ref, row_ref, cot_hbm,
    hid_hbm, wg_hbm, fg_hbm,
    feat, w, d, cot, own, xs, cols, scales, deg1, deg2, rdeg, rsc, hs, hT, part, e1, e2s, e2r, tot,
    hid, pushed, pushT, tt, zb, bfar, bnear, bside, u, yp, us, fin, g, w1, g1, w2, g2, w3, g4, gout, fg,
    in_sem, out_sem, s1_s, s1_r, x_s, x_r, z_s, z_r, d1_s, d1_r, d2_s, d2_r, rd_s, rd_r,
    e_s, e_r, zb_s, zb_r, b_s, b_r, yp_s, yp_r, f_s, f_r,
    w1_s, w1_r, w2_s, w2_r, w3_s, w3_r, w4_s, w4_r, w5_s, w5_r,
):
    row = lax.axis_index("row")
    q = lax.axis_index("rep")
    y = (row // 16) * 2 + q // 2
    x = (row // 4) % 4
    z = row % 4
    c = q % 2
    yh = row // 16
    yl = q // 2
    zp = z + 4 - q
    me8 = yh * 4 + q
    sent = []

    def remote(src, dst, ssem, rsem, to):
        return pltpu.make_async_remote_copy(
            src_ref=src, dst_ref=dst, send_sem=ssem, recv_sem=rsem, device_id=to, device_id_type=MESH
        )

    def send(src, dst, ssem, rsem, to, when=None):
        copy = remote(src, dst, ssem, rsem, to)
        if when is None:
            copy.start()
        else:
            pl.when(when)(copy.start)
        sent.append((copy, when))
        return copy

    loads = [
        pltpu.make_async_copy(src, dst, in_sem.at[n])
        for n, (src, dst) in enumerate(((feat_hbm, feat), (d_hbm, d), (w_hbm, w), (cot_hbm, cot)))
    ]
    for copy in loads:
        copy.start()

    barrier = pltpu.get_barrier_semaphore()
    place32 = y * 8 + z * 2 + c
    for n in range(1, 32):
        other = (place32 + n) % 32
        pl.semaphore_signal(
            barrier, inc=1, device_id=place(other // 8, x, (other // 2) % 4, other % 2), device_id_type=MESH
        )
    for n in range(1, 4):
        pl.semaphore_signal(barrier, inc=1, device_id=place(y, x + n, z, c), device_id_type=MESH)

    loads[0].wait()
    key0, key1 = key_ref[0], key_ref[1]
    for i in range(4):
        nodes = row * ROWS + i * BLK + lax.broadcasted_iota(jnp.int32, (BLK, FEAT), 0)
        feats = lax.broadcasted_iota(jnp.int32, (BLK, FEAT), 1)
        at = pl.ds(i * BLK, BLK)
        kept = keep_mask(nodes, feats, key0, key1)
        own[at, :] = jnp.where(kept, feat[at, :].astype(F32), 0.0).astype(BF16)
    cols[...] = col_ref[...]
    rdeg[0] = row_ref[...]
    pl.semaphore_wait(barrier, 34)

    same, other = yh * 4, 4 - yh * 4
    lead = ((yh + c) % 2) * 4
    rest = 4 - lead
    x1, x2, xo = (x + 1 + 2 * c) % 4, (x + 3 + 2 * c) % 4, (x + 2) % 4
    dev1, dev2 = place(y, x1, z, c), place(y, x2, z, c)
    pair = place(y, x, z + 1 + 2 * c, 1 - c)
    step = ROWS // CHUNKS

    def piece(panel, k):
        return xs.at[panel, pl.ds(k * step, step)]

    def own_piece(k):
        return own.at[pl.ds(k * step, step)]

    chunks = range(CHUNKS)
    got_same = [
        send(own_piece(k), piece(same + x, k), s1_s.at[0, k], s1_r.at[0, k], place(y, x, z + q, c), q != 0)
        for k in chunks
    ]
    got_other = [
        send(own_piece(k), piece(same + x, k), s1_s.at[1, k], s1_r.at[1, k], place(3 - y, x, z + c, c), yl == 1)
        for k in chunks
    ]

    d1 = [
        send(cols, deg1.at[n - 1], d1_s.at[n - 1], d1_r.at[n - 1], place(y, x + n, z, c))
        for n in range(1, 4)
    ]
    rd = [
        send(rdeg.at[0], rdeg.at[n], rd_s.at[n - 1], rd_r.at[n - 1], (row, (q + n) % 4))
        for n in range(1, 4)
    ]

    @pl.when(q == 0)
    def _():
        xs[same + x] = own[...]

    def wait_when(copy, when):
        pl.when(when)(copy.wait_recv)

    by1, by2 = [[], []], []
    for k in chunks:
        wait_when(got_same[k], q != 0)
        src = piece(same + x, k)
        send(src, src, s1_s.at[2, k], s1_r.at[1, k], place(y + 2, x, z, c), yl == 1)
        by2.append(send(src, src, x_s.at[2, k], x_r.at[2, k], dev2, c == 0))
        by1[0].append(send(src, src, x_s.at[0, k], x_r.at[0, k], dev1))
    for k in chunks:
        got_other[k].wait_recv()
        src = piece(other + x, k)
        send(src, src, x_s.at[2, k], x_r.at[2, k], dev2, c == 1)
        by1[1].append(send(src, src, x_s.at[1, k], x_r.at[1, k], dev1))

    for copy in d1:
        copy.wait_recv()
    deg2[0] = cols[...] + deg1[0] + deg1[1] + deg1[2]
    d2 = []
    for n in range(1, 8):
        o = (me8 + n) % 8
        o_q = o % 4
        to = place((o // 4) * 2 + o_q // 2, x, zp + o_q, o_q % 2)
        d2.append(send(deg2.at[0], deg2.at[n], d2_s.at[n - 1], d2_r.at[n - 1], to))

    onward, cross = [], [[], []]
    for k in chunks:
        by2[k].wait_recv()
        src = piece(lead + x1, k)
        onward.append(send(src, src, x_s.at[3, k], x_r.at[3, k], dev2))
    for k in chunks:
        src = piece(lead + x2, k)
        remote(src, src, x_s.at[0, k], x_r.at[c, k], dev1).wait_recv()
        cross[0].append(send(src, src, z_s.at[0, k], z_r.at[0, k], pair))

    for copy in rd:
        copy.wait_recv()
    by_rep = [rdeg[(q + 4 - s) % 4] for s in range(4)]
    row_scale = lax.rsqrt(1.0 + ((by_rep[0] + by_rep[1]) + (by_rep[2] + by_rep[3])))
    row_cols = jnp.concatenate([row_scale, row_scale], axis=0).T
    for i in range(4):
        rsc[i] = row_cols[:, i : i + 1]
    for copy in d2:
        copy.wait_recv()
    total = deg2[0]
    for n in range(1, 8):
        total = total + deg2[n]
    scales[...] = lax.rsqrt(1.0 + total)

    loads[1].wait()
    eye = lax.broadcasted_iota(jnp.int32, (BLK, BLK), 0) == lax.broadcasted_iota(jnp.int32, (BLK, BLK), 1)
    eye = jnp.where(eye, 1.0, 0.0)
    for l in range(32):
        flag = jnp.where(jnp.logical_and(q == 0, same + x == l // 4), 1.0, 0.0)
        scale = scales[pl.ds(l, 1), :]
        for i in range(4):
            block = d[pl.ds(i * BLK, BLK), pl.ds(l * BLK, BLK)].astype(F32)
            if i == l % 4:
                block = block + eye * flag
            d[pl.ds(i * BLK, BLK), pl.ds(l * BLK, BLK)] = (block * scale).astype(BF16)

    for k in chunks:
        onward[k].wait_recv()
        src = piece(lead + xo, k)
        cross[1].append(send(src, src, z_s.at[1, k], z_r.at[1, k], pair))

    def panel_cols(p):
        return pl.ds(pl.multiple_of(p * ROWS, ROWS), ROWS)

    def term(p):
        return jnp.dot(d[:, panel_cols(p)], xs[p], preferred_element_type=F32)

    acc = term(same + x) + term(other + x)
    acc = acc + term(lead + x1)
    acc = acc + term(lead + x2)
    acc = acc + term(lead + xo)
    for k in chunks:
        src = piece(rest + x2, k)
        remote(src, src, x_s.at[0, k], x_r.at[1 - c, k], dev1).wait_recv()
    acc = acc + term(rest + x2)
    for k in chunks:
        cross[0][k].wait_recv()
    acc = acc + term(rest + x1)
    for k in chunks:
        cross[1][k].wait_recv()
    acc = acc + term(rest + xo)
    hs[...] = acc.astype(BF16)
    loads[2].wait()

    half = ROWS // 2
    partner = place(y, x, z, 1 - c)
    chip = (row, (1 - yl) * 2 + c)

    def rows128(b):
        return pl.ds(pl.multiple_of(b * BLK, BLK), BLK)

    def project(b):
        part[rows128(b), :] = (
            jnp.dot(hs[rows128(b), :], w[...], preferred_element_type=F32) * 1.25
        ).astype(BF16)

    ec = [[], [], []]
    for b in range(2):
        project((1 - c) * 2 + b)
        ec[0].append(send(part.at[rows128((1 - c) * 2 + b)], e1.at[b], e_s.at[0, b], e_r.at[0, b], partner))
    project(c * 2)
    project(c * 2 + 1)
    for b in range(2):
        ec[0][b].wait_recv()
        e2s[b] = (part[rows128(c * 2 + b), :].astype(F32) + e1[b].astype(F32)).astype(BF16)
        ec[1].append(send(e2s.at[b], e2r.at[b], e_s.at[1, b], e_r.at[1, b], chip))
    hT[...] = acc.T.astype(BF16)
    loads[3].wait()

    def activate(i):
        at = rows128(i)
        r = rsc[i]
        pre = tot[at, :].astype(F32) * r
        s = 1.0 / (1.0 + jnp.exp(-pre))
        hid[at, :] = (pre * s).astype(BF16)
        grad = cot[at, :].astype(F32) * s * (1.0 + pre * (1.0 - s)) * r
        pushed[at, :] = grad.astype(BF16)
        pushT[:, at] = grad.T.astype(BF16)

    for b in range(2):
        ec[1][b].wait_recv()
        at = rows128(c * 2 + b)
        tot[at, :] = (e2s[b].astype(F32) + e2r[b].astype(F32)).astype(BF16)
        ec[2].append(send(tot.at[at], tot.at[at], e_s.at[2, b], e_r.at[2, b], partner))
    activate(c * 2)
    activate(c * 2 + 1)
    for b in range(2):
        ec[2][b].wait_recv()
        activate((1 - c) * 2 + b)
    hid_out = pltpu.make_async_copy(hid, hid_hbm, out_sem.at[0])
    hid_out.start()

    g[...] = jnp.dot(hT[...], pushed[...], preferred_element_type=F32) * 1.25
    place8 = y * 2 + c
    w1c = []
    for n in range(1, 8):
        o = (place8 + n) % 8
        src = g.at[pl.ds(pl.multiple_of(o * 32, 32), 32)]
        w1c.append(send(src, w1.at[n - 1], w1_s.at[n - 1], w1_r.at[n - 1], place(o // 2, x, z, o % 2)))

    def back(p):
        out = jnp.dot(pushT[...], d[:, panel_cols(p)], preferred_element_type=F32).astype(BF16)
        for j in range(4):
            tt[p, j] = out[:, j * BLK : (j + 1) * BLK]

    def add(*blocks):
        out = blocks[0].astype(F32)
        for block in blocks[1:]:
            out = out + block.astype(F32)
        return out.astype(BF16)

    blocks4 = range(4)
    zc, sidec, farc, nearc = [[], []], [[], []], [], []
    back(rest + xo)
    for j in blocks4:
        zc[0].append(send(tt.at[rest + xo, j], zb.at[0, j], zb_s.at[0, j], zb_r.at[0, j], pair))
    back(rest + x1)
    for j in blocks4:
        zc[1].append(send(tt.at[rest + x1, j], zb.at[1, j], zb_s.at[1, j], zb_r.at[1, j], pair))
    back(rest + x2)
    for j in blocks4:
        sidec[1].append(send(tt.at[rest + x2, j], bside.at[1, j], b_s.at[1, j], b_r.at[1, j], dev2))
    back(lead + xo)
    for j in blocks4:
        zc[0][j].wait_recv()
        tt[lead + xo, j] = add(tt[lead + xo, j], zb[0, j])
        farc.append(send(tt.at[lead + xo, j], bfar.at[j], b_s.at[2, j], b_r.at[2, j], dev1))
    back(lead + x2)
    for j in blocks4:
        zc[1][j].wait_recv()
        tt[lead + x2, j] = add(tt[lead + x2, j], zb[1, j])
        sidec[0].append(send(tt.at[lead + x2, j], bside.at[0, j], b_s.at[0, j], b_r.at[0, j], dev2))

    for copy in w1c:
        copy.wait_recv()
    at32 = pl.ds(pl.multiple_of(place8 * 32, 32), 32)
    out = g[at32, :]
    for n in range(7):
        out = out + w1[n]
    g1[...] = out
    w2c = []
    for n in range(1, 4):
        xt = (x + n) % 4
        src = g1.at[pl.ds(pl.multiple_of(xt * 8, 8), 8)]
        w2c.append(send(src, w2.at[n - 1], w2_s.at[n - 1], w2_r.at[n - 1], place(y, xt, z, c)))

    back(lead + x1)
    for j in blocks4:
        farc[j].wait_recv()
        tt[lead + x1, j] = add(tt[lead + x1, j], bfar[j])
        nearc.append(send(tt.at[lead + x1, j], bnear.at[j], b_s.at[3, j], b_r.at[3, j], dev1))
    back(lead + x)
    back(rest + x)

    for copy in w2c:
        copy.wait_recv()
    at8 = pl.ds(pl.multiple_of(x * 8, 8), 8)
    g2v = (g1[at8, :] + w2[0]) + (w2[1] + w2[2])
    g2[...] = g2v
    w3[z] = g2v
    w3c = [send(g2, w3.at[z], w3_s.at[n - 1], w3_r.at[n - 1], place(y, x, z + n, c)) for n in range(1, 4)]

    lead_h, rest_h = lead // 4, rest // 4
    for j in blocks4:
        sidec[1][j].wait_recv()
        u[rest_h, j] = add(tt[rest + x, j], bside[1, j])
    for j in blocks4:
        sidec[0][j].wait_recv()
        nearc[j].wait_recv()
        u[lead_h, j] = add(tt[lead + x, j], bside[0, j], bnear[j])

    ypc = [send(u.at[1 - yh, j], yp.at[j], yp_s.at[j], yp_r.at[j], place(y + 2, x, z, c), yl == 1) for j in blocks4]

    for copy in w3c:
        copy.wait_recv()
    g4[at8, :] = (w3[0] + w3[1]) + (w3[2] + w3[3])
    w4c = [
        send(g4.at[at8], g4.at[at8], w4_s.at[n - 1], w4_r.at[n - 1], place(y, x + n, z, c))
        for n in range(1, 4)
    ]

    slot = jnp.where(yl == 0, yh * 2 + q, 2 + q)
    is0 = q == 0
    for j in blocks4:
        to = place(2 * (1 - yh) + j // 2, x, zp, j % 2)
        send(u.at[1 - yh, j], fin.at[slot], f_s.at[1, j], f_r.at[slot], to, yl == 0)
    for j in blocks4:
        wait_when(ypc[j], yl == 1)

        @pl.when(yl == 1)
        def _():
            us[j] = add(u[yh, j], yp[j])

        @pl.when(yl == 0)
        def _():
            us[j] = u[yh, j]

        to = place(2 * yh + j // 2, x, zp, j % 2)
        send(us.at[j], fin.at[slot], f_s.at[0, j], f_r.at[slot], to, jnp.logical_not(is0) if j == 0 else None)

    @pl.when(is0)
    def _():
        fin[slot] = us[0]

    for copy in w4c:
        copy.wait_recv()
    gout[at32, :] = g4[...]
    w5c = []
    for n in range(1, 8):
        o = (place8 + n) % 8
        w5c.append(send(g4, gout.at[at32], w5_s.at[n - 1], w5_r.at[n - 1], place(o // 2, x, z, o % 2)))

    for n in range(6):
        copy = remote(us.at[0], fin.at[n], f_s.at[0, 0], f_r.at[n], (row, q))
        if n == 0 or n == 2:
            wait_when(copy, jnp.logical_not(jnp.logical_and(is0, slot == n)))
        else:
            copy.wait_recv()
    proj = fin[0].astype(F32)
    for n in range(1, 6):
        proj = proj + fin[n].astype(F32)
    proj = proj.T.astype(BF16)
    back_proj = lax.dot_general(proj, w[...], (((1,), (1,)), ((), ())), preferred_element_type=F32) * 1.25
    nodes = row * ROWS + q * BLK + lax.broadcasted_iota(jnp.int32, (BLK, FEAT), 0)
    feats = lax.broadcasted_iota(jnp.int32, (BLK, FEAT), 1)
    fg[...] = jnp.where(keep_mask(nodes, feats, key0, key1), back_proj, 0.0).astype(BF16)
    fg_out = pltpu.make_async_copy(fg, fg_hbm, out_sem.at[1])
    fg_out.start()
    for copy in w5c:
        copy.wait_recv()
    wg_out = pltpu.make_async_copy(gout, wg_hbm, out_sem.at[2])
    wg_out.start()
    for copy, when in sent:
        if when is None:
            copy.wait_send()
        else:
            pl.when(when)(copy.wait_send)
    hid_out.wait()
    fg_out.wait()
    wg_out.wait()


def layer(drop_key, features, weight, d, col, row, cotangent):
    dma = pltpu.SemaphoreType.DMA
    vmem = pltpu.VMEM
    any_spec = pl.BlockSpec(memory_space=pl.ANY)
    vmem_spec = pl.BlockSpec(memory_space=pltpu.VMEM)
    return pl.pallas_call(
        layer_kernel,
        out_shape=[
            jax.ShapeDtypeStruct((ROWS, FEAT), BF16),
            jax.ShapeDtypeStruct((FEAT, FEAT), F32),
            jax.ShapeDtypeStruct((BLK, FEAT), BF16),
        ],
        in_specs=[
            pl.BlockSpec(memory_space=pltpu.SMEM),
            any_spec, any_spec, any_spec, vmem_spec, vmem_spec, any_spec,
        ],
        out_specs=[any_spec, any_spec, any_spec],
        scratch_shapes=[
            vmem((ROWS, FEAT), BF16),
            vmem((FEAT, FEAT), BF16),
            vmem((ROWS, 32 * BLK), BF16),
            vmem((ROWS, FEAT), BF16),
            vmem((ROWS, FEAT), BF16),
            vmem((8, ROWS, FEAT), BF16),
            vmem((32, BLK), F32),
            vmem((32, BLK), F32),
            vmem((3, 32, BLK), F32),
            vmem((8, 32, BLK), F32),
            vmem((4, 4, BLK), F32),
            vmem((4, BLK, 1), F32),
            vmem((ROWS, FEAT), BF16),
            vmem((FEAT, ROWS), BF16),
            vmem((ROWS, FEAT), BF16),
            vmem((2, BLK, FEAT), BF16),
            vmem((2, BLK, FEAT), BF16),
            vmem((2, BLK, FEAT), BF16),
            vmem((ROWS, FEAT), BF16),
            vmem((ROWS, FEAT), BF16),
            vmem((ROWS, FEAT), BF16),
            vmem((FEAT, ROWS), BF16),
            vmem((8, 4, FEAT, BLK), BF16),
            vmem((2, 4, FEAT, BLK), BF16),
            vmem((4, FEAT, BLK), BF16),
            vmem((4, FEAT, BLK), BF16),
            vmem((2, 4, FEAT, BLK), BF16),
            vmem((2, 4, FEAT, BLK), BF16),
            vmem((4, FEAT, BLK), BF16),
            vmem((4, FEAT, BLK), BF16),
            vmem((6, FEAT, BLK), BF16),
            vmem((FEAT, FEAT), F32),
            vmem((7, 32, FEAT), F32),
            vmem((32, FEAT), F32),
            vmem((3, 8, FEAT), F32),
            vmem((8, FEAT), F32),
            vmem((4, 8, FEAT), F32),
            vmem((32, FEAT), F32),
            vmem((FEAT, FEAT), F32),
            vmem((BLK, FEAT), BF16),
            dma((4,)), dma((3,)),
            dma((3, CHUNKS)), dma((2, CHUNKS)),
            dma((4, CHUNKS)), dma((4, CHUNKS)),
            dma((2, CHUNKS)), dma((2, CHUNKS)),
            dma((3,)), dma((3,)), dma((7,)), dma((7,)), dma((3,)), dma((3,)),
            dma((3, 2)), dma((3, 2)),
            dma((2, 4)), dma((2, 4)), dma((4, 4)), dma((4, 4)),
            dma((4,)), dma((4,)), dma((2, 4)), dma((6,)),
            dma((7,)), dma((7,)), dma((3,)), dma((3,)), dma((3,)), dma((3,)),
            dma((3,)), dma((3,)), dma((7,)), dma((7,)),
        ],
        compiler_params=pltpu.CompilerParams(
            collective_id=0, has_side_effects=True, vmem_limit_bytes=48 << 20
        ),
        name="layer",
    )(drop_key, features, weight, d, col, row, cotangent)


def shards(features, weight, adj_tiles, block_cols, edge_keep, drop_key, cotangent):
    d, col, row = build(block_cols, edge_keep, adj_tiles)
    hidden, weight_grad, feature_grad = layer(drop_key, features, weight, d, col, row, cotangent)
    return (hidden, weight_grad, feature_grad)


def solution(mesh):
    in_specs = (
        P("row", None),
        P(),
        P("row", "rep", None, None),
        P("row", "rep"),
        P("row", "rep"),
        P(),
        P("row", None),
    )
    out_specs = (P("row", None), P(), P(("row", "rep"), None))
    return jax.shard_map(shards, mesh=mesh, in_specs=in_specs, out_specs=out_specs, check_vma=False)
```

time: 105 us -> 88 us (0.84)
  Pallas kernels: 93.7 us -> 77.8 us
  other arithmetic: 1.27 us -> 0 us
    pallas_call x1, Pallas kernels: 88.1 us -> 72.3 us  [layer(): pl.pallas_call(layer_kernel, out_shape=[jax.ShapeDtypeStruct((ROWS, FEAT)...]
    add x1 -> x0, other arithmetic: 1.27 us -> none  [shards(): idx = block_cols // 16 * 4 + block_cols % 4]
where the time goes in v2:
time: 88 us; the launch traced here: 87.6 us
  Pallas kernels  77.8 us (88%)
  local copies, waits for them, and re-layouts  9.08 us (10%)
    pallas_call x1, Pallas kernels, layer(): pl.pallas_call(layer_kernel, out_shape=[jax.ShapeDtypeStruct((ROWS, FEAT)...  72.3 us
    unnamed x17, local copies, waits for them, and re-layouts  9.08 us
    pallas_call x1, Pallas kernels, build(): pl.pallas_call(build_kernel, grid_spec=pltpu.PrefetchScalarGridSpec(num_s...  5.53 us

profile of v2, /device:TPU:1, one launch (start us, length us, event | category | flops | bytes accessed | tf_op | source)
XLA Modules:
  0.0 87.6 jit_solution(15892901822517867293)
XLA Ops:
  0.6 5.5 %build.1 = (bf16[512,4096]{1,0:T(8,128)(2,1)}, f32[32,128]{1,0:T(8,128)}, f32[4,128]{1,0:T(4,128)}) custom-call(s32[4,16]{1,0:T(4,128)} %blk_ref.1, s32[4,16]{1,0:T(4,128)} %keep_ref.1, bf16[4,16,128,128]{3,2,1,0:T(8,128)(2,1)} %tiles_ref.1), custom_call_target="tpu_custom_call" | custom-call | tf_op jit(solution)/shard_map/build/pallas_call | solution.py:53
  6.2 0.0 copy-start
  6.2 2.2 %copy-done = bf16[512,4096]{1,0:T(8,128)(2,1)S(1)} copy-done((bf16[512,4096]{1,0:T(8,128)(2,1)S(1)}, bf16[512,4096]{1,0:T(8,128)(2,1)}, u32[]{:S(2)}) %copy-start) | copy-done | bytes 4194328
  8.4 0.0 copy-start.1
  8.4 0.9 %copy-done.1 = bf16[512,256]{1,0:T(8,128)(2,1)S(1)} copy-done((bf16[512,256]{1,0:T(8,128)(2,1)S(1)}, bf16[512,256]{1,0:T(8,128)(2,1)}, u32[]{:S(2)}) %copy-start.1) | copy-done | bytes 262168
  9.3 0.0 copy-start.2
  9.3 0.9 %copy-done.2 = bf16[512,256]{1,0:T(8,128)(2,1)S(1)} copy-done((bf16[512,256]{1,0:T(8,128)(2,1)S(1)}, bf16[512,256]{1,0:T(8,128)(2,1)}, u32[]{:S(2)}) %copy-start.2) | copy-done | bytes 262168
  10.3 0.0 copy-start.3
  10.3 0.9 %copy-done.3 = bf16[256,256]{1,0:T(8,128)(2,1)S(1)} copy-done((bf16[256,256]{1,0:T(8,128)(2,1)S(1)}, bf16[256,256]{1,0:T(8,128)(2,1)}, u32[]{:S(2)}) %copy-start.3) | copy-done | bytes 131096
  11.2 0.0 copy-start.4
  11.2 0.7 copy-done.4
  11.9 0.0 copy-start.5
  11.9 0.7 copy-done.5
  12.6 0.0 copy-start.6
  12.6 0.7 copy-done.6
  13.2 72.3 %layer.1 = (bf16[512,256]{1,0:T(8,128)(2,1)S(1)}, f32[256,256]{1,0:T(8,128)S(1)}, bf16[128,256]{1,0:T(8,128)(2,1)S(1)}) custom-call(s32[2]{0:T(128)S(1)} %copy-done.6, bf16[512,256]{1,0:T(8,128)(2,1)S(1)} %copy-done.1, bf16[256,256]{1,0:T(8,128)(2,1)S(1)} %copy-done.3, bf16[512,4096]{1,0:T(8,128)(2,1)S(1)} %copy-done, f32[32,128]{1,0:T(8,128)S(1)} %copy-done.4, ...), custom_call_target="tpu_custom_call" | custom-call | tf_op jit(solution)/shard_map/layer/pallas_call | solution.py:468
  85.5 0.7 copy.13
  86.2 0.7 copy.14
  86.9 0.6 copy.15
Async XLA Ops:
  6.2 2.2 %copy-start = (bf16[512,4096]{1,0:T(8,128)(2,1)S(1)}, bf16[512,4096]{1,0:T(8,128)(2,1)}, u32[]{:S(2)}) copy-start(bf16[512,4096]{1,0:T(8,128)(2,1)} %get-tuple-element.6.d_hbm) | copy-start | bytes 12582916
  8.4 0.9 %copy-start.1 = (bf16[512,256]{1,0:T(8,128)(2,1)S(1)}, bf16[512,256]{1,0:T(8,128)(2,1)}, u32[]{:S(2)}) copy-start(bf16[512,256]{1,0:T(8,128)(2,1)} %feat_hbm.1) | copy-start | bytes 786436
  9.3 0.9 %copy-start.2 = (bf16[512,256]{1,0:T(8,128)(2,1)S(1)}, bf16[512,256]{1,0:T(8,128)(2,1)}, u32[]{:S(2)}) copy-start(bf16[512,256]{1,0:T(8,128)(2,1)} %cot_hbm.1) | copy-start | bytes 786436
  10.3 0.9 %copy-start.3 = (bf16[256,256]{1,0:T(8,128)(2,1)S(1)}, bf16[256,256]{1,0:T(8,128)(2,1)}, u32[]{:S(2)}) copy-start(bf16[256,256]{1,0:T(8,128)(2,1)} %w_hbm.1) | copy-start | bytes 393220
  11.2 0.7 copy-start.4
  11.9 0.7 copy-start.5
  12.6 0.7 copy-start.6

commit v3 on v2

--- a/solution.py
+++ b/solution.py
@@ -75,10 +75,10 @@
     key_ref, feat_hbm, w_hbm, d_hbm, col_ref, row_ref, cot_hbm,
     hid_hbm, wg_hbm, fg_hbm,
     feat, w, d, cot, own, xs, cols, scales, deg1, deg2, rdeg, rsc, hs, hT, part, e1, e2s, e2r, tot,
-    hid, pushed, pushT, tt, zb, bfar, bnear, bside, u, yp, us, fin, g, w1, g1, w2, g2, w3, g4, gout, fg,
+    hid, pushed, pushT, tt, zb, bfar, bnear, bside, u, yp, fin, g, w1, w2, w3, g4, fg,
     in_sem, out_sem, s1_s, s1_r, x_s, x_r, z_s, z_r, d1_s, d1_r, d2_s, d2_r, rd_s, rd_r,
     e_s, e_r, zb_s, zb_r, b_s, b_r, yp_s, yp_r, f_s, f_r,
-    w1_s, w1_r, w2_s, w2_r, w3_s, w3_r, w4_s, w4_r, w5_s, w5_r,
+    w1_s, w1_r, w2_s, w2_r, w3_s, w3_r, w4_s, w4_r,
 ):
     row = lax.axis_index("row")
     q = lax.axis_index("rep")
@@ -135,7 +135,7 @@
     rdeg[0] = row_ref[...]
     pl.semaphore_wait(barrier, 34)
 
-    same, other = yh * 4, 4 - yh * 4
+    same = yh * 4
     lead = ((yh + c) % 2) * 4
     rest = 4 - lead
     x1, x2, xo = (x + 1 + 2 * c) % 4, (x + 3 + 2 * c) % 4, (x + 2) % 4
@@ -150,12 +150,13 @@
         return own.at[pl.ds(k * step, step)]
 
     chunks = range(CHUNKS)
-    got_same = [
-        send(own_piece(k), piece(same + x, k), s1_s.at[0, k], s1_r.at[0, k], place(y, x, z + q, c), q != 0)
-        for k in chunks
-    ]
-    got_other = [
-        send(own_piece(k), piece(same + x, k), s1_s.at[1, k], s1_r.at[1, k], place(3 - y, x, z + c, c), yl == 1)
+    first = lead + x
+    last = rest + x
+    across = place(y + 2, x, z, c)
+    to_y = jnp.where(c == 0, y, 3 - y)
+    to_z = z + jnp.where(c == 0, q, 3 - 2 * yl)
+    got = [
+        send(own_piece(k), piece(same + x, k), s1_s.at[0, k], s1_r.at[0, k], place(to_y, x, to_z, c), q != 0)
         for k in chunks
     ]
 
@@ -172,21 +173,26 @@
     def _():
         xs[same + x] = own[...]
 
+    loads[1].wait()
+
+    @pl.when(q == 0)
+    def _():
+        eye = lax.broadcasted_iota(jnp.int32, (BLK, BLK), 0) == lax.broadcasted_iota(jnp.int32, (BLK, BLK), 1)
+        eye = jnp.where(eye, 1.0, 0.0)
+        for i in range(4):
+            at = pl.ds(i * BLK, BLK), pl.ds(pl.multiple_of(first * ROWS + i * BLK, BLK), BLK)
+            d[at] = (d[at].astype(F32) + eye).astype(BF16)
+
     def wait_when(copy, when):
         pl.when(when)(copy.wait_recv)
 
-    by1, by2 = [[], []], []
-    for k in chunks:
-        wait_when(got_same[k], q != 0)
-        src = piece(same + x, k)
-        send(src, src, s1_s.at[2, k], s1_r.at[1, k], place(y + 2, x, z, c), yl == 1)
-        by2.append(send(src, src, x_s.at[2, k], x_r.at[2, k], dev2, c == 0))
+    by1, by2, got_rest = [[], []], [], []
+    for k in chunks:
+        wait_when(got[k], q != 0)
+        src = piece(first, k)
+        by2.append(send(src, src, x_s.at[2, k], x_r.at[2, k], dev2))
         by1[0].append(send(src, src, x_s.at[0, k], x_r.at[0, k], dev1))
-    for k in chunks:
-        got_other[k].wait_recv()
-        src = piece(other + x, k)
-        send(src, src, x_s.at[2, k], x_r.at[2, k], dev2, c == 1)
-        by1[1].append(send(src, src, x_s.at[1, k], x_r.at[1, k], dev1))
+        got_rest.append(send(src, src, s1_s.at[1, k], s1_r.at[1, k], across))
 
     for copy in d1:
         copy.wait_recv()
@@ -204,9 +210,13 @@
         src = piece(lead + x1, k)
         onward.append(send(src, src, x_s.at[3, k], x_r.at[3, k], dev2))
     for k in chunks:
+        by1[0][k].wait_recv()
         src = piece(lead + x2, k)
-        remote(src, src, x_s.at[0, k], x_r.at[c, k], dev1).wait_recv()
         cross[0].append(send(src, src, z_s.at[0, k], z_r.at[0, k], pair))
+    for k in chunks:
+        got_rest[k].wait_recv()
+        src = piece(last, k)
+        by1[1].append(send(src, src, x_s.at[1, k], x_r.at[1, k], dev1))
 
     for copy in rd:
         copy.wait_recv()
@@ -222,19 +232,16 @@
         total = total + deg2[n]
     scales[...] = lax.rsqrt(1.0 + total)
 
-    loads[1].wait()
-    eye = lax.broadcasted_iota(jnp.int32, (BLK, BLK), 0) == lax.broadcasted_iota(jnp.int32, (BLK, BLK), 1)
-    eye = jnp.where(eye, 1.0, 0.0)
-    for l in range(32):
-        flag = jnp.where(jnp.logical_and(q == 0, same + x == l // 4), 1.0, 0.0)
-        scale = scales[pl.ds(l, 1), :]
-        for i in range(4):
-            block = d[pl.ds(i * BLK, BLK), pl.ds(l * BLK, BLK)].astype(F32)
-            if i == l % 4:
-                block = block + eye * flag
-            d[pl.ds(i * BLK, BLK), pl.ds(l * BLK, BLK)] = (block * scale).astype(BF16)
-
-    for k in chunks:
+    narrow = scales[...].astype(BF16)
+
+    def scale_panel(p):
+        for l in range(4 * p, 4 * p + 4):
+            at = pl.ds(l * BLK, BLK)
+            d[:, at] = d[:, at] * narrow[l : l + 1, :]
+
+    for k in chunks:
+        for p in range(8 * k // CHUNKS, 8 * (k + 1) // CHUNKS):
+            scale_panel(p)
         onward[k].wait_recv()
         src = piece(lead + xo, k)
         cross[1].append(send(src, src, z_s.at[1, k], z_r.at[1, k], pair))
@@ -245,17 +252,16 @@
     def term(p):
         return jnp.dot(d[:, panel_cols(p)], xs[p], preferred_element_type=F32)
 
-    acc = term(same + x) + term(other + x)
+    acc = term(first) + term(last)
     acc = acc + term(lead + x1)
     acc = acc + term(lead + x2)
     acc = acc + term(lead + xo)
     for k in chunks:
-        src = piece(rest + x2, k)
-        remote(src, src, x_s.at[0, k], x_r.at[1 - c, k], dev1).wait_recv()
-    acc = acc + term(rest + x2)
-    for k in chunks:
         cross[0][k].wait_recv()
     acc = acc + term(rest + x1)
+    for k in chunks:
+        by1[1][k].wait_recv()
+    acc = acc + term(rest + x2)
     for k in chunks:
         cross[1][k].wait_recv()
     acc = acc + term(rest + xo)
@@ -310,8 +316,9 @@
     hid_out = pltpu.make_async_copy(hid, hid_hbm, out_sem.at[0])
     hid_out.start()
 
-    g[...] = jnp.dot(hT[...], pushed[...], preferred_element_type=F32) * 1.25
+    g[...] = (jnp.dot(hT[...], pushed[...], preferred_element_type=F32) * 1.25).astype(BF16)
     place8 = y * 2 + c
+    at32 = pl.ds(pl.multiple_of(place8 * 32, 32), 32)
     w1c = []
     for n in range(1, 8):
         o = (place8 + n) % 8
@@ -340,6 +347,14 @@
     back(rest + x2)
     for j in blocks4:
         sidec[1].append(send(tt.at[rest + x2, j], bside.at[1, j], b_s.at[1, j], b_r.at[1, j], dev2))
+    for copy in w1c:
+        copy.wait_recv()
+    w2[x] = add(g[at32, :], *[w1[n] for n in range(7)])
+    w2c = [
+        send(w2.at[x], w2.at[x], w2_s.at[n - 1], w2_r.at[n - 1], place(y, x + n, z, c)) for n in range(1, 4)
+    ]
+
+    back(last)
     back(lead + xo)
     for j in blocks4:
         zc[0][j].wait_recv()
@@ -351,104 +366,63 @@
         tt[lead + x2, j] = add(tt[lead + x2, j], zb[1, j])
         sidec[0].append(send(tt.at[lead + x2, j], bside.at[0, j], b_s.at[0, j], b_r.at[0, j], dev2))
 
-    for copy in w1c:
-        copy.wait_recv()
-    at32 = pl.ds(pl.multiple_of(place8 * 32, 32), 32)
-    out = g[at32, :]
-    for n in range(7):
-        out = out + w1[n]
-    g1[...] = out
-    w2c = []
-    for n in range(1, 4):
-        xt = (x + n) % 4
-        src = g1.at[pl.ds(pl.multiple_of(xt * 8, 8), 8)]
-        w2c.append(send(src, w2.at[n - 1], w2_s.at[n - 1], w2_r.at[n - 1], place(y, xt, z, c)))
+    for copy in w2c:
+        copy.wait_recv()
+    w3[z] = add(w2[0], w2[1], w2[2], w2[3])
+    w3c = [
+        send(w3.at[z], w3.at[z], w3_s.at[n - 1], w3_r.at[n - 1], place(y, x, z + n, c)) for n in range(1, 4)
+    ]
+
+    ypc = []
+    for j in blocks4:
+        sidec[1][j].wait_recv()
+        u[1, j] = add(tt[last, j], bside[1, j])
+        ypc.append(send(u.at[1, j], yp.at[j], yp_s.at[j], yp_r.at[j], across))
 
     back(lead + x1)
     for j in blocks4:
         farc[j].wait_recv()
         tt[lead + x1, j] = add(tt[lead + x1, j], bfar[j])
         nearc.append(send(tt.at[lead + x1, j], bnear.at[j], b_s.at[3, j], b_r.at[3, j], dev1))
-    back(lead + x)
-    back(rest + x)
-
-    for copy in w2c:
-        copy.wait_recv()
-    at8 = pl.ds(pl.multiple_of(x * 8, 8), 8)
-    g2v = (g1[at8, :] + w2[0]) + (w2[1] + w2[2])
-    g2[...] = g2v
-    w3[z] = g2v
-    w3c = [send(g2, w3.at[z], w3_s.at[n - 1], w3_r.at[n - 1], place(y, x, z + n, c)) for n in range(1, 4)]
-
-    lead_h, rest_h = lead // 4, rest // 4
-    for j in blocks4:
-        sidec[1][j].wait_recv()
-        u[rest_h, j] = add(tt[rest + x, j], bside[1, j])
+    back(first)
+
+    for copy in w3c:
+        copy.wait_recv()
+    g4[at32, :] = add(w3[0], w3[1], w3[2], w3[3])
+    w4c = []
+    for n in range(1, 8):
+        o = (place8 + n) % 8
+        src = g4.at[at32]
+        w4c.append(send(src, src, w4_s.at[n - 1], w4_r.at[n - 1], place(o // 2, x, z, o % 2)))
+
+    half_of = (yh + c) % 2
     for j in blocks4:
         sidec[0][j].wait_recv()
         nearc[j].wait_recv()
-        u[lead_h, j] = add(tt[lead + x, j], bside[0, j], bnear[j])
-
-    ypc = [send(u.at[1 - yh, j], yp.at[j], yp_s.at[j], yp_r.at[j], place(y + 2, x, z, c), yl == 1) for j in blocks4]
-
-    for copy in w3c:
-        copy.wait_recv()
-    g4[at8, :] = (w3[0] + w3[1]) + (w3[2] + w3[3])
-    w4c = [
-        send(g4.at[at8], g4.at[at8], w4_s.at[n - 1], w4_r.at[n - 1], place(y, x + n, z, c))
-        for n in range(1, 4)
-    ]
-
-    slot = jnp.where(yl == 0, yh * 2 + q, 2 + q)
-    is0 = q == 0
-    for j in blocks4:
-        to = place(2 * (1 - yh) + j // 2, x, zp, j % 2)
-        send(u.at[1 - yh, j], fin.at[slot], f_s.at[1, j], f_r.at[slot], to, yl == 0)
-    for j in blocks4:
-        wait_when(ypc[j], yl == 1)
-
-        @pl.when(yl == 1)
-        def _():
-            us[j] = add(u[yh, j], yp[j])
-
-        @pl.when(yl == 0)
-        def _():
-            us[j] = u[yh, j]
-
-        to = place(2 * yh + j // 2, x, zp, j % 2)
-        send(us.at[j], fin.at[slot], f_s.at[0, j], f_r.at[slot], to, jnp.logical_not(is0) if j == 0 else None)
-
-    @pl.when(is0)
+        ypc[j].wait_recv()
+        u[0, j] = add(tt[first, j], bside[0, j], bnear[j], yp[j])
+        to = place(2 * half_of + j // 2, x, zp, j % 2)
+        send(u.at[0, j], fin.at[q], f_s.at[j], f_r.at[q], to, q != 0 if j == 0 else None)
+
+    @pl.when(q == 0)
     def _():
-        fin[slot] = us[0]
-
-    for copy in w4c:
-        copy.wait_recv()
-    gout[at32, :] = g4[...]
-    w5c = []
-    for n in range(1, 8):
-        o = (place8 + n) % 8
-        w5c.append(send(g4, gout.at[at32], w5_s.at[n - 1], w5_r.at[n - 1], place(o // 2, x, z, o % 2)))
-
-    for n in range(6):
-        copy = remote(us.at[0], fin.at[n], f_s.at[0, 0], f_r.at[n], (row, q))
-        if n == 0 or n == 2:
-            wait_when(copy, jnp.logical_not(jnp.logical_and(is0, slot == n)))
+        fin[0] = u[0, 0]
+
+    for n in range(4):
+        copy = remote(u.at[0, 0], fin.at[n], f_s.at[0], f_r.at[n], (row, q))
+        if n == 0:
+            wait_when(copy, q != 0)
         else:
             copy.wait_recv()
     proj = fin[0].astype(F32)
-    for n in range(1, 6):
+    for n in range(1, 4):
         proj = proj + fin[n].astype(F32)
-    proj = proj.T.astype(BF16)
-    back_proj = lax.dot_general(proj, w[...], (((1,), (1,)), ((), ())), preferred_element_type=F32) * 1.25
-    nodes = row * ROWS + q * BLK + lax.broadcasted_iota(jnp.int32, (BLK, FEAT), 0)
-    feats = lax.broadcasted_iota(jnp.int32, (BLK, FEAT), 1)
-    fg[...] = jnp.where(keep_mask(nodes, feats, key0, key1), back_proj, 0.0).astype(BF16)
+    fg[...] = proj.T.astype(BF16)
     fg_out = pltpu.make_async_copy(fg, fg_hbm, out_sem.at[1])
     fg_out.start()
-    for copy in w5c:
-        copy.wait_recv()
-    wg_out = pltpu.make_async_copy(gout, wg_hbm, out_sem.at[2])
+    for copy in w4c:
+        copy.wait_recv()
+    wg_out = pltpu.make_async_copy(g4, wg_hbm, out_sem.at[2])
     wg_out.start()
     for copy, when in sent:
         if when is None:
@@ -469,7 +443,7 @@
         layer_kernel,
         out_shape=[
             jax.ShapeDtypeStruct((ROWS, FEAT), BF16),
-            jax.ShapeDtypeStruct((FEAT, FEAT), F32),
+            jax.ShapeDtypeStruct((FEAT, FEAT), BF16),
             jax.ShapeDtypeStruct((BLK, FEAT), BF16),
         ],
         in_specs=[
@@ -508,38 +482,61 @@
             vmem((2, 4, FEAT, BLK), BF16),
             vmem((4, FEAT, BLK), BF16),
             vmem((4, FEAT, BLK), BF16),
-            vmem((6, FEAT, BLK), BF16),
-            vmem((FEAT, FEAT), F32),
-            vmem((7, 32, FEAT), F32),
-            vmem((32, FEAT), F32),
-            vmem((3, 8, FEAT), F32),
-            vmem((8, FEAT), F32),
-            vmem((4, 8, FEAT), F32),
-            vmem((32, FEAT), F32),
-            vmem((FEAT, FEAT), F32),
+            vmem((FEAT, FEAT), BF16),
+            vmem((7, 32, FEAT), BF16),
+            vmem((4, 32, FEAT), BF16),
+            vmem((4, 32, FEAT), BF16),
+            vmem((FEAT, FEAT), BF16),
             vmem((BLK, FEAT), BF16),
             dma((4,)), dma((3,)),
-            dma((3, CHUNKS)), dma((2, CHUNKS)),
+            dma((2, CHUNKS)), dma((2, CHUNKS)),
             dma((4, CHUNKS)), dma((4, CHUNKS)),
             dma((2, CHUNKS)), dma((2, CHUNKS)),
             dma((3,)), dma((3,)), dma((7,)), dma((7,)), dma((3,)), dma((3,)),
             dma((3, 2)), dma((3, 2)),
             dma((2, 4)), dma((2, 4)), dma((4, 4)), dma((4, 4)),
-            dma((4,)), dma((4,)), dma((2, 4)), dma((6,)),
+            dma((4,)), dma((4,)), dma((4,)), dma((4,)),
             dma((7,)), dma((7,)), dma((3,)), dma((3,)), dma((3,)), dma((3,)),
-            dma((3,)), dma((3,)), dma((7,)), dma((7,)),
+            dma((7,)), dma((7,)),
         ],
         compiler_params=pltpu.CompilerParams(
-            collective_id=0, has_side_effects=True, vmem_limit_bytes=48 << 20
+            collective_id=0, has_side_effects=True, vmem_limit_bytes=58 << 20
         ),
         name="layer",
     )(drop_key, features, weight, d, col, row, cotangent)
 
 
+def finish_kernel(key_ref, hid_ref, g_ref, proj_ref, w_ref, hid_out, wg_out, fg_out):
+    hid_out[...] = hid_ref[...]
+    wg_out[...] = g_ref[...].astype(F32)
+    back_proj = (
+        lax.dot_general(proj_ref[...], w_ref[...], (((1,), (1,)), ((), ())), preferred_element_type=F32) * 1.25
+    )
+    first = lax.axis_index("row") * ROWS + lax.axis_index("rep") * BLK
+    nodes = first + lax.broadcasted_iota(jnp.int32, (BLK, FEAT), 0)
+    feats = lax.broadcasted_iota(jnp.int32, (BLK, FEAT), 1)
+    kept = keep_mask(nodes, feats, key_ref[0], key_ref[1])
+    fg_out[...] = jnp.where(kept, back_proj, 0.0).astype(BF16)
+
+
+def finish(drop_key, hid, g, proj, weight):
+    return pl.pallas_call(
+        finish_kernel,
+        out_shape=[
+            jax.ShapeDtypeStruct((ROWS, FEAT), BF16),
+            jax.ShapeDtypeStruct((FEAT, FEAT), F32),
+            jax.ShapeDtypeStruct((BLK, FEAT), BF16),
+        ],
+        in_specs=[pl.BlockSpec(memory_space=pltpu.SMEM)] + [pl.BlockSpec(memory_space=pltpu.VMEM)] * 4,
+        out_specs=[pl.BlockSpec(memory_space=pltpu.VMEM)] * 3,
+        name="finish",
+    )(drop_key, hid, g, proj, weight)
+
+
 def shards(features, weight, adj_tiles, block_cols, edge_keep, drop_key, cotangent):
     d, col, row = build(block_cols, edge_keep, adj_tiles)
-    hidden, weight_grad, feature_grad = layer(drop_key, features, weight, d, col, row, cotangent)
-    return (hidden, weight_grad, feature_grad)
+    hidden, grad, proj = layer(drop_key, features, weight, d, col, row, cotangent)
+    return finish(drop_key, hidden, grad, proj, weight)
 
 
 def solution(mesh):

time: 88 us -> 72.5 us (0.82)
  local copies, waits for them, and re-layouts: 9.08 us -> 0 us
  Pallas kernels: 77.8 us -> 71.6 us
    unnamed x17 -> x0, local copies, waits for them, and re-layouts: 9.08 us -> none
    pallas_call x1, Pallas kernels: 72.3 us -> 64 us  [layer(): pl.pallas_call(layer_kernel, out_shape=[jax.ShapeDtypeStruct((ROWS, FEAT)...]
    pallas_call x0 -> x1, Pallas kernels: none -> 1.99 us  [finish(): pl.pallas_call(finish_kernel, out_shape=[jax.ShapeDtypeStruct((ROWS, FEAT...]
where the time goes in v3:
time: 72.5 us; the launch traced here: 72.2 us
  Pallas kernels  71.6 us (99%)
    pallas_call x1, Pallas kernels, layer(): pl.pallas_call(layer_kernel, out_shape=[jax.ShapeDtypeStruct((ROWS, FEAT)...  64 us
    pallas_call x1, Pallas kernels, build(): pl.pallas_call(build_kernel, grid_spec=pltpu.PrefetchScalarGridSpec(num_s...  5.53 us
    pallas_call x1, Pallas kernels, finish(): pl.pallas_call(finish_kernel, out_shape=[jax.ShapeDtypeStruct((ROWS, FEAT...  1.99 us

profile of v3, /device:TPU:1, one launch (start us, length us, event | category | flops | bytes accessed | tf_op | source)
XLA Modules:
  0.0 72.2 jit_solution(17676712110905862446)
XLA Ops:
  0.6 5.5 %build.1 = (bf16[512,4096]{1,0:T(8,128)(2,1)}, f32[32,128]{1,0:T(8,128)}, f32[4,128]{1,0:T(4,128)}) custom-call(s32[4,16]{1,0:T(4,128)} %blk_ref.1, s32[4,16]{1,0:T(4,128)} %keep_ref.1, bf16[4,16,128,128]{3,2,1,0:T(8,128)(2,1)} %tiles_ref.1), custom_call_target="tpu_custom_call" | custom-call | tf_op jit(solution)/shard_map/build/pallas_call | solution.py:53
  6.2 64.0 %layer.1 = (bf16[512,256]{1,0:T(8,128)(2,1)}, bf16[256,256]{1,0:T(8,128)(2,1)}, bf16[128,256]{1,0:T(8,128)(2,1)}) custom-call(s32[2]{0:T(128)} %key_ref.3, bf16[512,256]{1,0:T(8,128)(2,1)} %feat_hbm.1, bf16[256,256]{1,0:T(8,128)(2,1)} %w_ref.1, bf16[512,4096]{1,0:T(8,128)(2,1)} %get-tuple-element.9.d_hbm, f32[32,128]{1,0:T(8,128)} %get-tuple-element.10.col_ref, ...), custom_call_target="tpu_custom_call" | custom-call | tf_op jit(solution)/shard_map/layer/pallas_call | solution.py:442
  70.2 2.0 %finish.1 = (bf16[512,256]{1,0:T(8,128)(2,1)}, f32[256,256]{1,0:T(8,128)}, bf16[128,256]{1,0:T(8,128)(2,1)}) custom-call(s32[2]{0:T(128)} %key_ref.3, bf16[512,256]{1,0:T(8,128)(2,1)} %get-tuple-element.12.hid_ref, bf16[256,256]{1,0:T(8,128)(2,1)} %get-tuple-element.13.g_ref, bf16[128,256]{1,0:T(8,128)(2,1)} %get-tuple-element.14.proj_ref, ...), custom_call_target="tpu_custom_call" | custom-call | tf_op jit(solution)/shard_map/finish/pallas_call | solution.py:523

commit v4 on v3

--- a/solution.py
+++ b/solution.py
@@ -29,44 +29,41 @@
     return ((y // 2) * 16 + x * 4 + z, (y % 2) * 2 + c)
 
 
-def build_kernel(blk_ref, keep_ref, tiles_ref, d_ref, col_ref, row_ref):
-    i = pl.program_id(0)
-
-    @pl.when(i == 0)
-    def _():
-        col_ref[...] = jnp.zeros_like(col_ref)
-
+def build_kernel(blk_ref, keep_ref, tiles_hbm, d_ref, col_ref, row_ref, tiles, sem):
+    loads = [pltpu.make_async_copy(tiles_hbm.at[i], tiles.at[i], sem.at[i]) for i in range(4)]
+    for copy in loads:
+        copy.start()
+    col_ref[...] = jnp.zeros_like(col_ref)
     d_ref[...] = jnp.zeros_like(d_ref)
-    row_acc = jnp.zeros((BLK, BLK), F32)
-    for k in range(16):
-        col = blk_ref[i, k]
-        slot = (col >> 4) * 4 + (col & 3)
-        tile = tiles_ref[0, k].astype(F32) * keep_ref[i, k].astype(F32)
-        at = pl.ds(pl.multiple_of(slot * BLK, BLK), BLK)
-        d_ref[:, at] = (d_ref[:, at].astype(F32) + tile).astype(BF16)
-        col_ref[pl.ds(slot, 1), :] += jnp.sum(tile, axis=0, keepdims=True)
-        row_acc = row_acc + tile
-    row_ref[pl.ds(i, 1), :] = jnp.sum(row_acc.T, axis=0, keepdims=True)
+    for i in range(4):
+        loads[i].wait()
+        rows = pl.ds(i * BLK, BLK)
+        row_acc = jnp.zeros((BLK, BLK), F32)
+        for k in range(16):
+            col = blk_ref[i, k]
+            slot = (col >> 4) * 4 + (col & 3)
+            tile = tiles[i, k] * keep_ref[i, k].astype(BF16)
+            at = pl.ds(pl.multiple_of(slot * BLK, BLK), BLK)
+            d_ref[rows, at] = d_ref[rows, at] + tile
+            wide = tile.astype(F32)
+            col_ref[pl.ds(slot, 1), :] += jnp.sum(wide, axis=0, keepdims=True)
+            row_acc = row_acc + wide
+        row_ref[pl.ds(i, 1), :] = jnp.sum(row_acc.T, axis=0, keepdims=True)
 
 
 def build(cols, keep, tiles):
+    smem, vmem = pl.BlockSpec(memory_space=pltpu.SMEM), pl.BlockSpec(memory_space=pltpu.VMEM)
     return pl.pallas_call(
         build_kernel,
-        grid_spec=pltpu.PrefetchScalarGridSpec(
-            num_scalar_prefetch=2,
-            grid=(4,),
-            in_specs=[pl.BlockSpec((1, 16, BLK, BLK), lambda i, a, b: (i, 0, 0, 0))],
-            out_specs=[
-                pl.BlockSpec((BLK, 32 * BLK), lambda i, a, b: (i, 0)),
-                pl.BlockSpec((32, BLK), lambda i, a, b: (0, 0)),
-                pl.BlockSpec((4, BLK), lambda i, a, b: (0, 0)),
-            ],
-        ),
+        in_specs=[smem, smem, pl.BlockSpec(memory_space=pl.ANY)],
+        out_specs=[vmem, vmem, vmem],
         out_shape=[
             jax.ShapeDtypeStruct((ROWS, 32 * BLK), BF16),
             jax.ShapeDtypeStruct((32, BLK), F32),
             jax.ShapeDtypeStruct((4, BLK), F32),
         ],
+        scratch_shapes=[pltpu.VMEM((4, 16, BLK, BLK), BF16), pltpu.SemaphoreType.DMA((4,))],
+        compiler_params=pltpu.CompilerParams(vmem_limit_bytes=12 << 20),
         name="build",
     )(cols, keep, tiles)
 
@@ -252,10 +249,9 @@
     def term(p):
         return jnp.dot(d[:, panel_cols(p)], xs[p], preferred_element_type=F32)
 
-    acc = term(first) + term(last)
-    acc = acc + term(lead + x1)
-    acc = acc + term(lead + x2)
-    acc = acc + term(lead + xo)
+    lead4 = pl.ds(pl.multiple_of(lead * ROWS, ROWS), 4 * ROWS)
+    acc = jnp.dot(d[:, lead4], xs[pl.ds(lead, 4)].reshape(4 * ROWS, FEAT), preferred_element_type=F32)
+    acc = acc + term(last)
     for k in chunks:
         cross[0][k].wait_recv()
     acc = acc + term(rest + x1)
@@ -500,7 +496,7 @@
             dma((7,)), dma((7,)),
         ],
         compiler_params=pltpu.CompilerParams(
-            collective_id=0, has_side_effects=True, vmem_limit_bytes=58 << 20
+            collective_id=0, has_side_effects=True, vmem_limit_bytes=24 << 20
         ),
         name="layer",
     )(drop_key, features, weight, d, col, row, cotangent)
@@ -529,11 +525,16 @@
         ],
         in_specs=[pl.BlockSpec(memory_space=pltpu.SMEM)] + [pl.BlockSpec(memory_space=pltpu.VMEM)] * 4,
         out_specs=[pl.BlockSpec(memory_space=pltpu.VMEM)] * 3,
+        compiler_params=pltpu.CompilerParams(vmem_limit_bytes=4 << 20),
         name="finish",
     )(drop_key, hid, g, proj, weight)
 
 
 def shards(features, weight, adj_tiles, block_cols, edge_keep, drop_key, cotangent):
+    features, weight, adj_tiles, block_cols, edge_keep, drop_key, cotangent = (
+        pltpu.with_memory_space_constraint(a, pltpu.HBM)
+        for a in (features, weight, adj_tiles, block_cols, edge_keep, drop_key, cotangent)
+    )
     d, col, row = build(block_cols, edge_keep, adj_tiles)
     hidden, grad, proj = layer(drop_key, features, weight, d, col, row, cotangent)
     return finish(drop_key, hidden, grad, proj, weight)

time: 72.5 us -> 70.1 us (0.967)
  Pallas kernels: 71.6 us -> 69.3 us
    pallas_call x1, Pallas kernels: 5.53 us -> 3.23 us  [build(): pl.pallas_call(build_kernel, in_specs=[smem, smem, pl.BlockSpec(memory_sp...]
where the time goes in v4:
time: 70.1 us; the launch traced here: 69.9 us
  Pallas kernels  69.3 us (99%)
    pallas_call x1, Pallas kernels, layer(): pl.pallas_call(layer_kernel, out_shape=[jax.ShapeDtypeStruct((ROWS, FEAT)...  64.2 us
    pallas_call x1, Pallas kernels, build(): pl.pallas_call(build_kernel, in_specs=[smem, smem, pl.BlockSpec(memory_sp...  3.23 us
    pallas_call x1, Pallas kernels, finish(): pl.pallas_call(finish_kernel, out_shape=[jax.ShapeDtypeStruct((ROWS, FEAT...  1.82 us

profile of v4, /device:TPU:1, one launch (start us, length us, event | category | flops | bytes accessed | tf_op | source)
XLA Modules:
  0.0 69.9 jit_solution(229773051660139270)
XLA Ops:
  0.6 3.2 %build.1 = (bf16[512,4096]{1,0:T(8,128)(2,1)S(1)}, f32[32,128]{1,0:T(8,128)S(1)}, f32[4,128]{1,0:T(4,128)S(1)}) custom-call(s32[4,16]{1,0:T(4,128)} %blk_ref.1, s32[4,16]{1,0:T(4,128)} %keep_ref.1, bf16[4,16,128,128]{3,2,1,0:T(8,128)(2,1)} %tiles_hbm.1), custom_call_target="tpu_custom_call" | custom-call | tf_op jit(solution)/shard_map/build/pallas_call | solution.py:56
  3.9 64.2 %layer.1 = (bf16[512,256]{1,0:T(8,128)(2,1)S(1)}, bf16[256,256]{1,0:T(8,128)(2,1)S(1)}, bf16[128,256]{1,0:T(8,128)(2,1)S(1)}) custom-call(s32[2]{0:T(128)} %key_ref.3, bf16[512,256]{1,0:T(8,128)(2,1)} %feat_hbm.1, bf16[256,256]{1,0:T(8,128)(2,1)} %w_ref.1, bf16[512,4096]{1,0:T(8,128)(2,1)S(1)} %get-tuple-element.9.d_hbm, ...), custom_call_target="tpu_custom_call" | custom-call | tf_op jit(solution)/shard_map/layer/pallas_call | solution.py:438
  68.1 1.8 %finish.1 = (bf16[512,256]{1,0:T(8,128)(2,1)}, f32[256,256]{1,0:T(8,128)}, bf16[128,256]{1,0:T(8,128)(2,1)}) custom-call(s32[2]{0:T(128)} %key_ref.3, bf16[512,256]{1,0:T(8,128)(2,1)S(1)} %get-tuple-element.12.hid_ref, bf16[256,256]{1,0:T(8,128)(2,1)S(1)} %get-tuple-element.13.g_ref, bf16[128,256]{1,0:T(8,128)(2,1)S(1)} %get-tuple-element.14.proj_ref, ...), custom_call_target="tpu_custom_call" | custom-call | tf_op jit(solution)/shard_map/finish/pallas_call | solution.py:519

commit v5 on v4

--- a/solution.py
+++ b/solution.py
@@ -29,12 +29,29 @@
     return ((y // 2) * 16 + x * 4 + z, (y % 2) * 2 + c)
 
 
-def build_kernel(blk_ref, keep_ref, tiles_hbm, d_ref, col_ref, row_ref, tiles, sem):
+def build_kernel(
+    key_ref, blk_ref, keep_ref, feat_hbm, tiles_hbm, own_ref, gate_ref, d_ref, col_ref, row_ref, feat, tiles, sem
+):
     loads = [pltpu.make_async_copy(tiles_hbm.at[i], tiles.at[i], sem.at[i]) for i in range(4)]
-    for copy in loads:
+    loads.append(pltpu.make_async_copy(feat_hbm, feat, sem.at[4]))
+    loads[4].start()
+    for copy in loads[:4]:
         copy.start()
     col_ref[...] = jnp.zeros_like(col_ref)
     d_ref[...] = jnp.zeros_like(d_ref)
+
+    first_node = lax.axis_index("row") * ROWS
+
+    def kept(start):
+        nodes = first_node + start + lax.broadcasted_iota(jnp.int32, (BLK, FEAT), 0)
+        feats = lax.broadcasted_iota(jnp.int32, (BLK, FEAT), 1)
+        return keep_mask(nodes, feats, key_ref[0], key_ref[1])
+
+    gate_ref[...] = jnp.where(kept(lax.axis_index("rep") * BLK), 1.0, 0.0)
+    loads[4].wait()
+    for i in range(4):
+        at = pl.ds(i * BLK, BLK)
+        own_ref[at, :] = jnp.where(kept(i * BLK), feat[at, :].astype(F32), 0.0).astype(BF16)
     for i in range(4):
         loads[i].wait()
         rows = pl.ds(i * BLK, BLK)
@@ -51,29 +68,36 @@
         row_ref[pl.ds(i, 1), :] = jnp.sum(row_acc.T, axis=0, keepdims=True)
 
 
-def build(cols, keep, tiles):
+def build(drop_key, cols, keep, features, tiles):
     smem, vmem = pl.BlockSpec(memory_space=pltpu.SMEM), pl.BlockSpec(memory_space=pltpu.VMEM)
+    any_spec = pl.BlockSpec(memory_space=pl.ANY)
     return pl.pallas_call(
         build_kernel,
-        in_specs=[smem, smem, pl.BlockSpec(memory_space=pl.ANY)],
-        out_specs=[vmem, vmem, vmem],
+        in_specs=[smem, smem, smem, any_spec, any_spec],
+        out_specs=[vmem] * 5,
         out_shape=[
+            jax.ShapeDtypeStruct((ROWS, FEAT), BF16),
+            jax.ShapeDtypeStruct((BLK, FEAT), F32),
             jax.ShapeDtypeStruct((ROWS, 32 * BLK), BF16),
             jax.ShapeDtypeStruct((32, BLK), F32),
             jax.ShapeDtypeStruct((4, BLK), F32),
         ],
-        scratch_shapes=[pltpu.VMEM((4, 16, BLK, BLK), BF16), pltpu.SemaphoreType.DMA((4,))],
+        scratch_shapes=[
+            pltpu.VMEM((ROWS, FEAT), BF16),
+            pltpu.VMEM((4, 16, BLK, BLK), BF16),
+            pltpu.SemaphoreType.DMA((5,)),
+        ],
         compiler_params=pltpu.CompilerParams(vmem_limit_bytes=12 << 20),
         name="build",
-    )(cols, keep, tiles)
+    )(drop_key, cols, keep, features, tiles)
 
 
 def layer_kernel(
-    key_ref, feat_hbm, w_hbm, d_hbm, col_ref, row_ref, cot_hbm,
-    hid_hbm, wg_hbm, fg_hbm,
-    feat, w, d, cot, own, xs, cols, scales, deg1, deg2, rdeg, rsc, hs, hT, part, e1, e2s, e2r, tot,
-    hid, pushed, pushT, tt, zb, bfar, bnear, bside, u, yp, fin, g, w1, w2, w3, g4, fg,
-    in_sem, out_sem, s1_s, s1_r, x_s, x_r, z_s, z_r, d1_s, d1_r, d2_s, d2_r, rd_s, rd_r,
+    own, w_hbm, d_hbm, col_ref, row_ref, cot_hbm,
+    hid, wg_ref, proj_ref, w,
+    d, cot, xs, cols, scales, deg1, deg2, rdeg, rsc, hs, hT, part, e1, e2s, e2r, tot,
+    pushed, pushT, tt, zb, bfar, bnear, bside, u, yp, fin, g, w1, w2, w3, g4,
+    in_sem, s1_s, s1_r, x_s, x_r, z_s, z_r, d1_s, d1_r, d2_s, d2_r, rd_s, rd_r,
     e_s, e_r, zb_s, zb_r, b_s, b_r, yp_s, yp_r, f_s, f_r,
     w1_s, w1_r, w2_s, w2_r, w3_s, w3_r, w4_s, w4_r,
 ):
@@ -105,7 +129,7 @@
 
     loads = [
         pltpu.make_async_copy(src, dst, in_sem.at[n])
-        for n, (src, dst) in enumerate(((feat_hbm, feat), (d_hbm, d), (w_hbm, w), (cot_hbm, cot)))
+        for n, (src, dst) in enumerate(((d_hbm, d), (w_hbm, w), (cot_hbm, cot)))
     ]
     for copy in loads:
         copy.start()
@@ -120,14 +144,6 @@
     for n in range(1, 4):
         pl.semaphore_signal(barrier, inc=1, device_id=place(y, x + n, z, c), device_id_type=MESH)
 
-    loads[0].wait()
-    key0, key1 = key_ref[0], key_ref[1]
-    for i in range(4):
-        nodes = row * ROWS + i * BLK + lax.broadcasted_iota(jnp.int32, (BLK, FEAT), 0)
-        feats = lax.broadcasted_iota(jnp.int32, (BLK, FEAT), 1)
-        at = pl.ds(i * BLK, BLK)
-        kept = keep_mask(nodes, feats, key0, key1)
-        own[at, :] = jnp.where(kept, feat[at, :].astype(F32), 0.0).astype(BF16)
     cols[...] = col_ref[...]
     rdeg[0] = row_ref[...]
     pl.semaphore_wait(barrier, 34)
@@ -170,7 +186,7 @@
     def _():
         xs[same + x] = own[...]
 
-    loads[1].wait()
+    loads[0].wait()
 
     @pl.when(q == 0)
     def _():
@@ -180,6 +196,14 @@
             at = pl.ds(i * BLK, BLK), pl.ds(pl.multiple_of(first * ROWS + i * BLK, BLK), BLK)
             d[at] = (d[at].astype(F32) + eye).astype(BF16)
 
+    def drain():
+        for copy, when in sent:
+            if when is None:
+                copy.wait_send()
+            else:
+                pl.when(when)(copy.wait_send)
+        sent.clear()
+
     def wait_when(copy, when):
         pl.when(when)(copy.wait_recv)
 
@@ -262,7 +286,7 @@
         cross[1][k].wait_recv()
     acc = acc + term(rest + xo)
     hs[...] = acc.astype(BF16)
-    loads[2].wait()
+    loads[1].wait()
 
     half = ROWS // 2
     partner = place(y, x, z, 1 - c)
@@ -286,8 +310,12 @@
         ec[0][b].wait_recv()
         e2s[b] = (part[rows128(c * 2 + b), :].astype(F32) + e1[b].astype(F32)).astype(BF16)
         ec[1].append(send(e2s.at[b], e2r.at[b], e_s.at[1, b], e_r.at[1, b], chip))
+    e_sent = sent[-4:]
+    del sent[-4:]
+    drain()
+    sent.extend(e_sent)
     hT[...] = acc.T.astype(BF16)
-    loads[3].wait()
+    loads[2].wait()
 
     def activate(i):
         at = rows128(i)
@@ -309,8 +337,6 @@
     for b in range(2):
         ec[2][b].wait_recv()
         activate((1 - c) * 2 + b)
-    hid_out = pltpu.make_async_copy(hid, hid_hbm, out_sem.at[0])
-    hid_out.start()
 
     g[...] = (jnp.dot(hT[...], pushed[...], preferred_element_type=F32) * 1.25).astype(BF16)
     place8 = y * 2 + c
@@ -356,6 +382,12 @@
         zc[0][j].wait_recv()
         tt[lead + xo, j] = add(tt[lead + xo, j], zb[0, j])
         farc.append(send(tt.at[lead + xo, j], bfar.at[j], b_s.at[2, j], b_r.at[2, j], dev1))
+    ypc = []
+    for j in blocks4:
+        sidec[1][j].wait_recv()
+        u[1, j] = add(tt[last, j], bside[1, j])
+        ypc.append(send(u.at[1, j], yp.at[j], yp_s.at[j], yp_r.at[j], across))
+
     back(lead + x2)
     for j in blocks4:
         zc[1][j].wait_recv()
@@ -368,12 +400,6 @@
     w3c = [
         send(w3.at[z], w3.at[z], w3_s.at[n - 1], w3_r.at[n - 1], place(y, x, z + n, c)) for n in range(1, 4)
     ]
-
-    ypc = []
-    for j in blocks4:
-        sidec[1][j].wait_recv()
-        u[1, j] = add(tt[last, j], bside[1, j])
-        ypc.append(send(u.at[1, j], yp.at[j], yp_s.at[j], yp_r.at[j], across))
 
     back(lead + x1)
     for j in blocks4:
@@ -413,24 +439,14 @@
     proj = fin[0].astype(F32)
     for n in range(1, 4):
         proj = proj + fin[n].astype(F32)
-    fg[...] = proj.T.astype(BF16)
-    fg_out = pltpu.make_async_copy(fg, fg_hbm, out_sem.at[1])
-    fg_out.start()
+    proj_ref[...] = proj.T.astype(BF16)
     for copy in w4c:
         copy.wait_recv()
-    wg_out = pltpu.make_async_copy(g4, wg_hbm, out_sem.at[2])
-    wg_out.start()
-    for copy, when in sent:
-        if when is None:
-            copy.wait_send()
-        else:
-            pl.when(when)(copy.wait_send)
-    hid_out.wait()
-    fg_out.wait()
-    wg_out.wait()
-
-
-def layer(drop_key, features, weight, d, col, row, cotangent):
+    wg_ref[...] = g4[...]
+    drain()
+
+
+def layer(own, weight, d, col, row, cotangent):
     dma = pltpu.SemaphoreType.DMA
     vmem = pltpu.VMEM
     any_spec = pl.BlockSpec(memory_space=pl.ANY)
@@ -441,17 +457,12 @@
             jax.ShapeDtypeStruct((ROWS, FEAT), BF16),
             jax.ShapeDtypeStruct((FEAT, FEAT), BF16),
             jax.ShapeDtypeStruct((BLK, FEAT), BF16),
+            jax.ShapeDtypeStruct((FEAT, FEAT), BF16),
         ],
-        in_specs=[
-            pl.BlockSpec(memory_space=pltpu.SMEM),
-            any_spec, any_spec, any_spec, vmem_spec, vmem_spec, any_spec,
-        ],
-        out_specs=[any_spec, any_spec, any_spec],
+        in_specs=[vmem_spec, any_spec, any_spec, vmem_spec, vmem_spec, any_spec],
+        out_specs=[vmem_spec] * 4,
         scratch_shapes=[
-            vmem((ROWS, FEAT), BF16),
-            vmem((FEAT, FEAT), BF16),
             vmem((ROWS, 32 * BLK), BF16),
-            vmem((ROWS, FEAT), BF16),
             vmem((ROWS, FEAT), BF16),
             vmem((8, ROWS, FEAT), BF16),
             vmem((32, BLK), F32),
@@ -468,7 +479,6 @@
             vmem((2, BLK, FEAT), BF16),
             vmem((ROWS, FEAT), BF16),
             vmem((ROWS, FEAT), BF16),
-            vmem((ROWS, FEAT), BF16),
             vmem((FEAT, ROWS), BF16),
             vmem((8, 4, FEAT, BLK), BF16),
             vmem((2, 4, FEAT, BLK), BF16),
@@ -483,8 +493,7 @@
             vmem((4, 32, FEAT), BF16),
             vmem((4, 32, FEAT), BF16),
             vmem((FEAT, FEAT), BF16),
-            vmem((BLK, FEAT), BF16),
-            dma((4,)), dma((3,)),
+            dma((3,)),
             dma((2, CHUNKS)), dma((2, CHUNKS)),
             dma((4, CHUNKS)), dma((4, CHUNKS)),
             dma((2, CHUNKS)), dma((2, CHUNKS)),
@@ -499,23 +508,19 @@
             collective_id=0, has_side_effects=True, vmem_limit_bytes=24 << 20
         ),
         name="layer",
-    )(drop_key, features, weight, d, col, row, cotangent)
-
-
-def finish_kernel(key_ref, hid_ref, g_ref, proj_ref, w_ref, hid_out, wg_out, fg_out):
+    )(own, weight, d, col, row, cotangent)
+
+
+def finish_kernel(hid_ref, g_ref, proj_ref, w_ref, gate_ref, hid_out, wg_out, fg_out):
     hid_out[...] = hid_ref[...]
     wg_out[...] = g_ref[...].astype(F32)
     back_proj = (
         lax.dot_general(proj_ref[...], w_ref[...], (((1,), (1,)), ((), ())), preferred_element_type=F32) * 1.25
     )
-    first = lax.axis_index("row") * ROWS + lax.axis_index("rep") * BLK
-    nodes = first + lax.broadcasted_iota(jnp.int32, (BLK, FEAT), 0)
-    feats = lax.broadcasted_iota(jnp.int32, (BLK, FEAT), 1)
-    kept = keep_mask(nodes, feats, key_ref[0], key_ref[1])
-    fg_out[...] = jnp.where(kept, back_proj, 0.0).astype(BF16)
-
-
-def finish(drop_key, hid, g, proj, weight):
+    fg_out[...] = jnp.where(gate_ref[...] > 0.0, back_proj, 0.0).astype(BF16)
+
+
+def finish(hid, g, proj, weight, gate):
     return pl.pallas_call(
         finish_kernel,
         out_shape=[
@@ -523,11 +528,11 @@
             jax.ShapeDtypeStruct((FEAT, FEAT), F32),
             jax.ShapeDtypeStruct((BLK, FEAT), BF16),
         ],
-        in_specs=[pl.BlockSpec(memory_space=pltpu.SMEM)] + [pl.BlockSpec(memory_space=pltpu.VMEM)] * 4,
+        in_specs=[pl.BlockSpec(memory_space=pltpu.VMEM)] * 5,
         out_specs=[pl.BlockSpec(memory_space=pltpu.VMEM)] * 3,
         compiler_params=pltpu.CompilerParams(vmem_limit_bytes=4 << 20),
         name="finish",
-    )(drop_key, hid, g, proj, weight)
+    )(hid, g, proj, weight, gate)
 
 
 def shards(features, weight, adj_tiles, block_cols, edge_keep, drop_key, cotangent):
@@ -535,9 +540,9 @@
         pltpu.with_memory_space_constraint(a, pltpu.HBM)
         for a in (features, weight, adj_tiles, block_cols, edge_keep, drop_key, cotangent)
     )
-    d, col, row = build(block_cols, edge_keep, adj_tiles)
-    hidden, grad, proj = layer(drop_key, features, weight, d, col, row, cotangent)
-    return finish(drop_key, hidden, grad, proj, weight)
+    own, gate, d, col, row = build(drop_key, block_cols, edge_keep, features, adj_tiles)
+    hidden, grad, proj, kept_weight = layer(own, weight, d, col, row, cotangent)
+    return finish(hidden, grad, proj, kept_weight, gate)
 
 
 def solution(mesh):

time: 70.1 us -> 67.4 us (0.961)
  Pallas kernels: 69.3 us -> 66.6 us
    pallas_call x1, Pallas kernels: 64.2 us -> 62.3 us  [layer(): pl.pallas_call(layer_kernel, out_shape=[jax.ShapeDtypeStruct((ROWS, FEAT)...]
    pallas_call x1, Pallas kernels: 1.82 us -> 0.9 us  [finish(): pl.pallas_call(finish_kernel, out_shape=[jax.ShapeDtypeStruct((ROWS, FEAT...]
where the time goes in v5:
time: 67.4 us; the launch traced here: 67.2 us
  Pallas kernels  66.6 us (99%)
    pallas_call x1, Pallas kernels, layer(): pl.pallas_call(layer_kernel, out_shape=[jax.ShapeDtypeStruct((ROWS, FEAT)...  62.3 us
    pallas_call x1, Pallas kernels, build(): pl.pallas_call(build_kernel, in_specs=[smem, smem, smem, any_spec, any_sp...  3.39 us

profile of v5, /device:TPU:1, one launch (start us, length us, event | category | flops | bytes accessed | tf_op | source)
XLA Modules:
  0.0 67.2 jit_solution(10520134245976449191)
XLA Ops:
  0.6 3.4 %build.1 = (bf16[512,256]{1,0:T(8,128)(2,1)S(1)}, f32[128,256]{1,0:T(8,128)S(1)}, bf16[512,4096]{1,0:T(8,128)(2,1)S(1)}, f32[32,128]{1,0:T(8,128)S(1)}, f32[4,128]{1,0:T(4,128)S(1)}) custom-call(s32[2]{0:T(128)} %key_ref.1, s32[4,16]{1,0:T(4,128)} %blk_ref.1, s32[4,16]{1,0:T(4,128)} %keep_ref.1, bf16[512,256]{1,0:T(8,128)(2,1)} %feat_hbm.1, ...), custom_call_target="tpu_custom_call" | custom-call | tf_op jit(solution)/shard_map/build/pallas_call | solution.py:74
  4.0 62.3 %layer.1 = (bf16[512,256]{1,0:T(8,128)(2,1)S(1)}, bf16[256,256]{1,0:T(8,128)(2,1)S(1)}, bf16[128,256]{1,0:T(8,128)(2,1)S(1)}, bf16[256,256]{1,0:T(8,128)(2,1)S(1)}) custom-call(bf16[512,256]{1,0:T(8,128)(2,1)S(1)} %get-tuple-element.12.own, bf16[256,256]{1,0:T(8,128)(2,1)} %w_hbm.1, bf16[512,4096]{1,0:T(8,128)(2,1)S(1)} %get-tuple-element.13.d_hbm, ...), custom_call_target="tpu_custom_call" | custom-call | tf_op jit(solution)/shard_map/layer/pallas_call | solution.py:454
  66.3 0.9 %finish.1 = (bf16[512,256]{1,0:T(8,128)(2,1)}, f32[256,256]{1,0:T(8,128)}, bf16[128,256]{1,0:T(8,128)(2,1)}) custom-call(bf16[512,256]{1,0:T(8,128)(2,1)S(1)} %get-tuple-element.16.hid_ref, bf16[256,256]{1,0:T(8,128)(2,1)S(1)} %get-tuple-element.17.g_ref, bf16[128,256]{1,0:T(8,128)(2,1)S(1)} %get-tuple-element.18.proj_ref, ...), custom_call_target="tpu_custom_call" | custom-call | tf_op jit(solution)/shard_map/finish/pallas_call | solution.py:524

commit v6 on v5

--- a/solution.py
+++ b/solution.py
@@ -388,12 +388,6 @@
         u[1, j] = add(tt[last, j], bside[1, j])
         ypc.append(send(u.at[1, j], yp.at[j], yp_s.at[j], yp_r.at[j], across))
 
-    back(lead + x2)
-    for j in blocks4:
-        zc[1][j].wait_recv()
-        tt[lead + x2, j] = add(tt[lead + x2, j], zb[1, j])
-        sidec[0].append(send(tt.at[lead + x2, j], bside.at[0, j], b_s.at[0, j], b_r.at[0, j], dev2))
-
     for copy in w2c:
         copy.wait_recv()
     w3[z] = add(w2[0], w2[1], w2[2], w2[3])
@@ -401,13 +395,17 @@
         send(w3.at[z], w3.at[z], w3_s.at[n - 1], w3_r.at[n - 1], place(y, x, z + n, c)) for n in range(1, 4)
     ]
 
+    back(lead + x2)
+    for j in blocks4:
+        zc[1][j].wait_recv()
+        tt[lead + x2, j] = add(tt[lead + x2, j], zb[1, j])
+        sidec[0].append(send(tt.at[lead + x2, j], bside.at[0, j], b_s.at[0, j], b_r.at[0, j], dev2))
+
     back(lead + x1)
     for j in blocks4:
         farc[j].wait_recv()
         tt[lead + x1, j] = add(tt[lead + x1, j], bfar[j])
         nearc.append(send(tt.at[lead + x1, j], bnear.at[j], b_s.at[3, j], b_r.at[3, j], dev1))
-    back(first)
-
     for copy in w3c:
         copy.wait_recv()
     g4[at32, :] = add(w3[0], w3[1], w3[2], w3[3])
@@ -417,6 +415,8 @@
         src = g4.at[at32]
         w4c.append(send(src, src, w4_s.at[n - 1], w4_r.at[n - 1], place(o // 2, x, z, o % 2)))
 
+    back(first)
+
     half_of = (yh + c) % 2
     for j in blocks4:
         sidec[0][j].wait_recv()
@@ -429,6 +429,11 @@
     @pl.when(q == 0)
     def _():
         fin[0] = u[0, 0]
+
+    f_sent = sent[-4:]
+    del sent[-4:]
+    drain()
+    sent.extend(f_sent)
 
     for n in range(4):
         copy = remote(u.at[0, 0], fin.at[n], f_s.at[0], f_r.at[n], (row, q))

time: 67.4 us -> 67 us (level)
  no operation moved by 1% of the time
where the time goes in v6:
time: 67 us; the launch traced here: 66.8 us
  Pallas kernels  66.2 us (99%)
    pallas_call x1, Pallas kernels, layer(): pl.pallas_call(layer_kernel, out_shape=[jax.ShapeDtypeStruct((ROWS, FEAT)...  61.9 us
    pallas_call x1, Pallas kernels, build(): pl.pallas_call(build_kernel, in_specs=[smem, smem, smem, any_spec, any_sp...  3.39 us

profile of v6, /device:TPU:1, one launch (start us, length us, event | category | flops | bytes accessed | tf_op | source)
XLA Modules:
  0.0 66.8 jit_solution(9620263413839474559)
XLA Ops:
  0.6 3.4 %build.1 = (bf16[512,256]{1,0:T(8,128)(2,1)S(1)}, f32[128,256]{1,0:T(8,128)S(1)}, bf16[512,4096]{1,0:T(8,128)(2,1)S(1)}, f32[32,128]{1,0:T(8,128)S(1)}, f32[4,128]{1,0:T(4,128)S(1)}) custom-call(s32[2]{0:T(128)} %key_ref.1, s32[4,16]{1,0:T(4,128)} %blk_ref.1, s32[4,16]{1,0:T(4,128)} %keep_ref.1, bf16[512,256]{1,0:T(8,128)(2,1)} %feat_hbm.1, ...), custom_call_target="tpu_custom_call" | custom-call | tf_op jit(solution)/shard_map/build/pallas_call | solution.py:74
  4.0 61.9 %layer.1 = (bf16[512,256]{1,0:T(8,128)(2,1)S(1)}, bf16[256,256]{1,0:T(8,128)(2,1)S(1)}, bf16[128,256]{1,0:T(8,128)(2,1)S(1)}, bf16[256,256]{1,0:T(8,128)(2,1)S(1)}) custom-call(bf16[512,256]{1,0:T(8,128)(2,1)S(1)} %get-tuple-element.12.own, bf16[256,256]{1,0:T(8,128)(2,1)} %w_hbm.1, bf16[512,4096]{1,0:T(8,128)(2,1)S(1)} %get-tuple-element.13.d_hbm, ...), custom_call_target="tpu_custom_call" | custom-call | tf_op jit(solution)/shard_map/layer/pallas_call | solution.py:459
  65.9 0.9 %finish.1 = (bf16[512,256]{1,0:T(8,128)(2,1)}, f32[256,256]{1,0:T(8,128)}, bf16[128,256]{1,0:T(8,128)(2,1)}) custom-call(bf16[512,256]{1,0:T(8,128)(2,1)S(1)} %get-tuple-element.16.hid_ref, bf16[256,256]{1,0:T(8,128)(2,1)S(1)} %get-tuple-element.17.g_ref, bf16[128,256]{1,0:T(8,128)(2,1)S(1)} %get-tuple-element.18.proj_ref, ...), custom_call_target="tpu_custom_call" | custom-call | tf_op jit(solution)/shard_map/finish/pallas_call | solution.py:529

commit v7 on v6

--- a/solution.py
+++ b/solution.py
@@ -338,6 +338,22 @@
         ec[2][b].wait_recv()
         activate((1 - c) * 2 + b)
 
+    def back(p):
+        out = jnp.dot(pushT[...], d[:, panel_cols(p)], preferred_element_type=F32).astype(BF16)
+        for j in range(4):
+            tt[p, j] = out[:, j * BLK : (j + 1) * BLK]
+
+    def add(*blocks):
+        out = blocks[0].astype(F32)
+        for block in blocks[1:]:
+            out = out + block.astype(F32)
+        return out.astype(BF16)
+
+    blocks4 = range(4)
+    zc, sidec, farc, nearc = [[], []], [[], []], [], []
+    back(rest + xo)
+    for j in blocks4:
+        zc[0].append(send(tt.at[rest + xo, j], zb.at[0, j], zb_s.at[0, j], zb_r.at[0, j], pair))
     g[...] = (jnp.dot(hT[...], pushed[...], preferred_element_type=F32) * 1.25).astype(BF16)
     place8 = y * 2 + c
     at32 = pl.ds(pl.multiple_of(place8 * 32, 32), 32)
@@ -347,22 +363,6 @@
         src = g.at[pl.ds(pl.multiple_of(o * 32, 32), 32)]
         w1c.append(send(src, w1.at[n - 1], w1_s.at[n - 1], w1_r.at[n - 1], place(o // 2, x, z, o % 2)))
 
-    def back(p):
-        out = jnp.dot(pushT[...], d[:, panel_cols(p)], preferred_element_type=F32).astype(BF16)
-        for j in range(4):
-            tt[p, j] = out[:, j * BLK : (j + 1) * BLK]
-
-    def add(*blocks):
-        out = blocks[0].astype(F32)
-        for block in blocks[1:]:
-            out = out + block.astype(F32)
-        return out.astype(BF16)
-
-    blocks4 = range(4)
-    zc, sidec, farc, nearc = [[], []], [[], []], [], []
-    back(rest + xo)
-    for j in blocks4:
-        zc[0].append(send(tt.at[rest + xo, j], zb.at[0, j], zb_s.at[0, j], zb_r.at[0, j], pair))
     back(rest + x1)
     for j in blocks4:
         zc[1].append(send(tt.at[rest + x1, j], zb.at[1, j], zb_s.at[1, j], zb_r.at[1, j], pair))

time: 67 us -> 66.6 us (level)
  no operation moved by 1% of the time
where the time goes in v7:
time: 66.6 us; the launch traced here: 66.5 us
  Pallas kernels  65.8 us (99%)
    pallas_call x1, Pallas kernels, layer(): pl.pallas_call(layer_kernel, out_shape=[jax.ShapeDtypeStruct((ROWS, FEAT)...  61.5 us
    pallas_call x1, Pallas kernels, build(): pl.pallas_call(build_kernel, in_specs=[smem, smem, smem, any_spec, any_sp...  3.4 us

profile of v7, /device:TPU:1, one launch (start us, length us, event | category | flops | bytes accessed | tf_op | source)
XLA Modules:
  0.0 66.5 jit_solution(2856168256418826348)
XLA Ops:
  0.6 3.4 %build.1 = (bf16[512,256]{1,0:T(8,128)(2,1)S(1)}, f32[128,256]{1,0:T(8,128)S(1)}, bf16[512,4096]{1,0:T(8,128)(2,1)S(1)}, f32[32,128]{1,0:T(8,128)S(1)}, f32[4,128]{1,0:T(4,128)S(1)}) custom-call(s32[2]{0:T(128)} %key_ref.1, s32[4,16]{1,0:T(4,128)} %blk_ref.1, s32[4,16]{1,0:T(4,128)} %keep_ref.1, bf16[512,256]{1,0:T(8,128)(2,1)} %feat_hbm.1, ...), custom_call_target="tpu_custom_call" | custom-call | tf_op jit(solution)/shard_map/build/pallas_call | solution.py:74
  4.0 61.5 %layer.1 = (bf16[512,256]{1,0:T(8,128)(2,1)S(1)}, bf16[256,256]{1,0:T(8,128)(2,1)S(1)}, bf16[128,256]{1,0:T(8,128)(2,1)S(1)}, bf16[256,256]{1,0:T(8,128)(2,1)S(1)}) custom-call(bf16[512,256]{1,0:T(8,128)(2,1)S(1)} %get-tuple-element.12.own, bf16[256,256]{1,0:T(8,128)(2,1)} %w_hbm.1, bf16[512,4096]{1,0:T(8,128)(2,1)S(1)} %get-tuple-element.13.d_hbm, ...), custom_call_target="tpu_custom_call" | custom-call | tf_op jit(solution)/shard_map/layer/pallas_call | solution.py:459
  65.6 0.9 %finish.1 = (bf16[512,256]{1,0:T(8,128)(2,1)}, f32[256,256]{1,0:T(8,128)}, bf16[128,256]{1,0:T(8,128)(2,1)}) custom-call(bf16[512,256]{1,0:T(8,128)(2,1)S(1)} %get-tuple-element.16.hid_ref, bf16[256,256]{1,0:T(8,128)(2,1)S(1)} %get-tuple-element.17.g_ref, bf16[128,256]{1,0:T(8,128)(2,1)S(1)} %get-tuple-element.18.proj_ref, ...), custom_call_target="tpu_custom_call" | custom-call | tf_op jit(solution)/shard_map/finish/pallas_call | solution.py:529
